TPU v7x, 32 devices: a whole 2x2x4 slice. The times are simulated.
32 devices in a mesh: ctx: 8 (over z, core), tp: 4 (over y, x).
Axes of the slice: x: 2, y: 2, z: 4, core: 2. Of those that a mesh axis runs over, the one named last changes fastest.
Arguments:
- queries: bfloat16 [4096, 4096], P('ctx', 'tp'), may hold values from -140 to 140
- key_vecs: bfloat16 [4096, 1024], P('ctx', 'tp'), may hold values from -6 to 6
- value_vecs: bfloat16 [4096, 1024], P('ctx', 'tp'), may hold values from -6 to 6
- out_grad: bfloat16 [4096, 4096], P('ctx', 'tp'), may hold values from -6 to 6
- doc_ids: int32 [32], replicated, may hold values from 0 to 9, never falling along the last dimension, each value on 1 to 8 neighbouring positions
Outputs:
- attended: bfloat16 [4096, 4096], P('ctx', 'tp')
- query_grad: bfloat16 [4096, 4096], P('ctx', 'tp')
- key_grad: bfloat16 [4096, 1024], P('ctx', 'tp')
- value_grad: bfloat16 [4096, 1024], P('ctx', 'tp')
Inputs may be any that keep to these rules, and one draw needn't show every extreme that they name: doc_ids never fall along the sequence; each document covers 1 to 8 blocks and one covers exactly 8.
All inputs are finite; a program needn't handle non-finite values.
Results may differ from a plain program's by a relative error of at most 0.0075.
Values may be sent and summed in bfloat16 or wider, within the bound.
No kernel may reach another device: no remote copies, remote signals or barrier semaphores. Data moves between devices by JAX's collectives and lax.ppermute only.
A program may use at most 64 MiB of HBM per device.

v0:
```python
import jax
import jax.numpy as jnp
from jax import lax
from jax.sharding import PartitionSpec as P

QH = 32
KVH = 8
HD = 128
BLK = 128
REACH = 2


negative_fill = -1e30


def from_behind(block, axis, distance):
    devices = range(lax.axis_size(axis))
    route = [(i - distance, i) for i in devices if i - distance in devices]
    return lax.ppermute(block, axis, route)


def body(queries, key_vecs, value_vecs, out_grad, doc_ids):
    length_dev = queries.shape[0]
    kv_heads = key_vecs.shape[1] // HD
    group_size = QH // KVH
    scale_factor = HD ** (-0.5)
    blocks_dev = length_dev // BLK
    ctx_index = lax.axis_index("ctx")
    query_split = queries.reshape(length_dev, kv_heads, group_size, HD)
    grad_split = out_grad.reshape(length_dev, kv_heads, group_size, HD)
    own_pair = jnp.stack([key_vecs, value_vecs])
    windows = [own_pair]
    for offset in range(1, REACH + 1):
        windows.append(from_behind(own_pair, "ctx", offset))
    docs_pad = jnp.concatenate([jnp.full((REACH * blocks_dev,), -1, jnp.int32), doc_ids])
    query_docs = jnp.repeat(
        lax.dynamic_slice_in_dim(doc_ids, ctx_index * blocks_dev, blocks_dev, 0), BLK
    )
    query_pos = ctx_index * length_dev + jnp.arange(length_dev, dtype=jnp.int32)
    masks = []
    lives = []
    scores = []
    for offset in range(REACH + 1):
        key_docs = jnp.repeat(
            lax.dynamic_slice_in_dim(
                docs_pad, (ctx_index - offset + REACH) * blocks_dev, blocks_dev, 0
            ),
            BLK,
        )
        key_pos = (ctx_index - offset) * length_dev + jnp.arange(length_dev, dtype=jnp.int32)
        allowed = (
            (query_docs[:, None] == key_docs[None, :])
            & (key_pos[None, :] <= query_pos[:, None])
            & (key_pos[None, :] >= 0)
        )
        live = jnp.any(allowed)
        key_split = windows[offset][0].reshape(length_dev, kv_heads, HD)

        def score_fn(key_split=key_split):
            return (
                jnp.einsum(
                    "qhgd,khd->hgqk", query_split, key_split, preferred_element_type=jnp.float32
                )
                * scale_factor
            )

        if offset == 0:
            scores.append(score_fn())
        else:
            scores.append(score_fn())
        masks.append(allowed)
        lives.append(live)
    highest = jnp.max(
        jnp.stack(
            [
                jnp.max(jnp.where(masks[o], scores[o], negative_fill), axis=-1)
                for o in range(REACH + 1)
            ]
        ),
        axis=0,
    )[..., None]
    total = sum(
        (
            jnp.sum(jnp.where(masks[o], jnp.exp(scores[o] - highest), 0.0), axis=-1, keepdims=True)
            for o in range(REACH + 1)
        )
    )
    lse = highest + jnp.log(total)
    probs = [jnp.where(masks[o], jnp.exp(scores[o] - lse), 0.0) for o in range(REACH + 1)]
    probs16 = [piece_p.astype(jnp.bfloat16) for piece_p in probs]
    out_blank = jnp.zeros((length_dev, kv_heads, group_size, HD), jnp.float32)
    output = out_blank
    for offset in range(REACH + 1):
        value_split = windows[offset][1].reshape(length_dev, kv_heads, HD)

        def apply_fn(offset=offset, value_split=value_split):
            return jnp.einsum(
                "hgqk,khd->qhgd", probs16[offset], value_split, preferred_element_type=jnp.float32
            )

        if offset == 0:
            output = apply_fn()
        else:
            output = output + apply_fn()
    output16 = output.astype(jnp.bfloat16)
    delta = jnp.sum(grad_split.astype(jnp.float32) * output16.astype(jnp.float32), axis=-1)
    delta_hgq = jnp.transpose(delta, (1, 2, 0))[..., None]
    query_acc = out_blank
    partials = []
    for offset in range(REACH + 1):
        key_split = windows[offset][0].reshape(length_dev, kv_heads, HD)
        value_split = windows[offset][1].reshape(length_dev, kv_heads, HD)

        def back_fn(offset=offset, key_split=key_split, value_split=value_split):
            dprobs = jnp.einsum(
                "qhgd,khd->hgqk", grad_split, value_split, preferred_element_type=jnp.float32
            )
            dscores = (probs[offset] * (dprobs - delta_hgq)).astype(jnp.bfloat16)
            query_term = (
                jnp.einsum("hgqk,khd->qhgd", dscores, key_split, preferred_element_type=jnp.float32)
                * scale_factor
            )
            key_term = (
                jnp.einsum(
                    "hgqk,qhgd->khd", dscores, query_split, preferred_element_type=jnp.float32
                )
                * scale_factor
            )
            value_term = jnp.einsum(
                "hgqk,qhgd->khd", probs16[offset], grad_split, preferred_element_type=jnp.float32
            )
            stacked = jnp.stack(
                [
                    key_term.reshape(length_dev, kv_heads * HD),
                    value_term.reshape(length_dev, kv_heads * HD),
                ]
            )
            return (query_term, stacked)

        if offset == 0:
            query_term, stacked = back_fn()
        else:
            query_term, stacked = back_fn()
        query_acc = query_acc + query_term
        partials.append(stacked)
    returned = jnp.zeros_like(partials[0])
    for offset in range(REACH, 0, -1):
        returned = from_behind(returned + partials[offset], "ctx", -1)
    summed = partials[0] + returned
    attended = output16.reshape(length_dev, kv_heads * group_size * HD)
    query_grad = query_acc.astype(jnp.bfloat16).reshape(length_dev, kv_heads * group_size * HD)
    key_grad = summed[0].astype(jnp.bfloat16)
    value_grad = summed[1].astype(jnp.bfloat16)
    return (attended, query_grad, key_grad, value_grad)


def solution(mesh):
    placed = (P("ctx", "tp"), P("ctx", "tp"), P("ctx", "tp"), P("ctx", "tp"), P())
    return jax.shard_map(
        body,
        mesh=mesh,
        in_specs=placed,
        out_specs=(P("ctx", "tp"), P("ctx", "tp"), P("ctx", "tp"), P("ctx", "tp")),
        check_vma=False,
    )
```

profile of v0, /device:TPU:25, one launch (start us, length us, event | category | flops | bytes accessed | tf_op | source)
XLA Modules:
  0.0 116.9 jit_solution(6287935741299456450)
XLA Ops:
  0.6 1.1 copy.51
  1.7 1.1 copy.52
  2.8 0.8 pad_maximum_fusion.1
  3.7 1.3 %collective-permute-start.1 = (bf16[2,512,256]{1,2,0:T(8,128)(2,1)}, bf16[2,512,256]{1,2,0:T(8,128)(2,1)}, u32[]{:S(2)}, u32[]{:S(2)}) collective-permute-start(bf16[2,512,256]{1,2,0:T(8,128)(2,1)} %pad_maximum_fusion.1), channel_id=1, source_target_pairs={{0,8},{4,12},{8,16},{12,20},{16,24},{20,28},{1,9},{5,13},{9,17},{1... | collective-permute-start | bytes 1572872 | tf_op jit(solution)/shard_map/ppermute | solution.py:19
  5.0 1.3 %collective-permute-start = (bf16[2,512,256]{1,2,0:T(8,128)(2,1)}, bf16[2,512,256]{1,2,0:T(8,128)(2,1)}, u32[]{:S(2)}, u32[]{:S(2)}) collective-permute-start(bf16[2,512,256]{1,2,0:T(8,128)(2,1)} %pad_maximum_fusion.1), channel_id=1, source_target_pairs={{0,4},{4,8},{8,12},{12,16},{16,20},{20,24},{24,28},{1,5},{5,9},{9,... | collective-permute-start | bytes 1572872 | tf_op jit(solution)/shard_map/ppermute | solution.py:19
  6.3 0.9 pad_dynamic-slice_fusion.1
  7.4 1.1 and_and_fusion.1
  8.5 1.0 reshape_squeeze_stack.8
  9.5 1.0 reshape_squeeze_stack.9
  10.5 1.5 %copy.138 = bf16[512,1024]{0,1:T(8,128)(2,1)S(1)} copy(bf16[512,1024]{1,0:T(8,128)(2,1)} %param.5) | data formatting | bytes 2097152 | tf_op jit(solution)/shard_map/reshape | solution.py:29
  12.2 0.9 copy.93
  13.1 1.5 %copy.61 = bf16[512,1024]{0,1:T(8,128)(2,1)S(1)} copy(bf16[512,1024]{1,0:T(8,128)(2,1)} %param.8) | data formatting | bytes 2097152 | tf_op args[3]
  14.6 1.6 %fusion.18 = (f32[2,4,512]{2,1,0:T(4,128)S(1)}, f32[2,512,512,4]{2,1,3,0:T(8,128)S(1)}) fusion(pred[512,512]{0,1:T(8,128)(4,1)S(1)} %get-tuple-element.23, bf16[512,2,128,1]{0,2,3,1:T(8,128)(2,1)S(1)} %copy.101, bf16[512,2,4,128]{0,3,2,1:T(8,128)(2,1)S(1)} %bitcast.243), kind=kOutput, calls=%fused_computation.30 | convolution fusion | flops 543158272 | bytes 9977856 | tf_op jit(solution)/shard_map/qhgd,khd->hgqk/dot_general | solution.py:61
  16.2 2.5 %collective-permute-done.1 = bf16[2,512,256]{1,2,0:T(8,128)(2,1)} collective-permute-done((bf16[2,512,256]{1,2,0:T(8,128)(2,1)}, bf16[2,512,256]{1,2,0:T(8,128)(2,1)}, u32[]{:S(2)}, u32[]{:S(2)}) %collective-permute-start.1) | collective-permute-done | bytes 524320 | tf_op jit(solution)/shard_map/ppermute | solution.py:19
  18.7 1.4 %fusion.44 = (bf16[1,512,256]{1,2,0:T(8,128)(2,1)S(1)}, bf16[1,512,256]{1,2,0:T(8,128)(2,1)S(1)}) fusion(bf16[2,512,256]{1,2,0:T(8,128)(2,1)} %collective-permute-done.1), kind=kLoop, calls=%fused_computation.82 | loop fusion | bytes 1048576 | tf_op jit(solution)/shard_map/slice | solution.py:94
  20.1 1.6 %fusion.6 = (f32[2,4,512]{2,1,0:T(4,128)S(1)}, f32[2,512,512,4]{2,1,3,0:T(8,128)S(1)}) fusion(pred[512,512]{0,1:T(8,128)(4,1)S(1)} %get-tuple-element.22, bf16[512,2,128,1]{0,2,3,1:T(8,128)(2,1)S(1)} %bitcast.257, bf16[512,2,4,128]{0,3,2,1:T(8,128)(2,1)S(1)} %bitcast.244), kind=kOutput, calls=%fused_computation.12 | convolution fusion | flops 543158272 | bytes 9977856 | tf_op jit(solution)/shard_map/qhgd,khd->hgqk/dot_general | solution.py:61
  21.7 1.1 fusion.45
  22.8 4.8 %fusion.12 = (f32[2,4,512]{2,1,0:T(4,128)S(1)}, f32[2,512,512,4]{2,1,3,0:T(8,128)}) fusion(pred[512,512]{0,1:T(8,128)(4,1)S(1)} %get-tuple-element.21, bf16[512,2,128,1]{0,2,3,1:T(8,128)(2,1)S(1)} %bitcast.259, bf16[512,2,4,128]{0,3,2,1:T(8,128)(2,1)S(1)} %bitcast.245), kind=kOutput, calls=%fused_computation.21 | convolution fusion | flops 543158272 | bytes 9977856 | tf_op jit(solution)/shard_map/qhgd,khd->hgqk/dot_general | solution.py:61
  27.6 7.4 %fusion.15 = (f32[2,4,512]{2,1,0:T(4,128)S(1)}, f32[2,4,512]{2,1,0:T(4,128)S(1)}, f32[2,4,512]{2,1,0:T(4,128)S(1)}) fusion(f32[2,512,512,4]{2,1,3,0:T(8,128)} %get-tuple-element.33, f32[2,4,512]{2,1,0:T(4,128)S(1)} %bitcast.275, pred[512,512]{0,1:T(8,128)(4,1)S(1)} %get-tuple-element.21, f32[2,512,512,4]{2,1,3,0:T(8,128)S(1)} %get-tuple-element.29, ...), kind=kLoop, calls=%fused_computation.24 | loop fusion | flops 25153536 | bytes 26017792 | tf_op jit(solution)/shard_map/reduce_sum | solution.py:84
  35.1 2.8 %fusion.33 = f32[2,512,128,1]{1,2,3,0:T(8,128)} fusion(bf16[512,2,4,128]{0,3,2,1:T(8,128)(2,1)S(1)} %bitcast.250, f32[2,512,512,4]{2,1,3,0:T(8,128)S(1)} %get-tuple-element.29, f32[2,4,512]{2,1,0:T(4,128)S(1)} %bitcast.282, pred[512,512]{0,1:T(8,128)(4,1)S(1)} %get-tuple-element.22), kind=kOutput, calls=%fused_computation.77 | convolution fusion | flops 545259520 | bytes 10240000 | tf_op jit(solution)/shard_map/hgqk,qhgd->khd/dot_general | solution.py:129
  37.8 5.3 %fusion.36 = f32[2,512,128,1]{1,2,3,0:T(8,128)S(1)} fusion(bf16[512,2,4,128]{0,3,2,1:T(8,128)(2,1)S(1)} %bitcast.251, f32[2,512,512,4]{2,1,3,0:T(8,128)} %get-tuple-element.33, f32[2,4,512]{2,1,0:T(4,128)S(1)} %bitcast.283, pred[512,512]{0,1:T(8,128)(4,1)S(1)} %get-tuple-element.21), kind=kOutput, calls=%fused_computation.78 | convolution fusion | flops 545259520 | bytes 10240000 | tf_op jit(solution)/shard_map/hgqk,qhgd->khd/dot_general | solution.py:129
  43.1 2.2 %fusion.42 = f32[2,4,512,128]{2,3,1,0:T(8,128)S(1)} fusion(bf16[512,2,128,1]{0,2,3,1:T(8,128)(2,1)S(1)} %copy-done.11, f32[2,512,512,4]{2,1,3,0:T(8,128)S(1)} %get-tuple-element.31, f32[2,4,512]{2,1,0:T(4,128)S(1)} %bitcast.284, pred[512,512]{0,1:T(8,128)(4,1)S(1)} %get-tuple-element.23), kind=kOutput, calls=%fused_computation.81 | convolution fusion | flops 545259520 | bytes 11026432 | tf_op jit(solution)/shard_map/hgqk,khd->qhgd/dot_general | solution.py:97
  45.3 5.3 %fusion.38 = f32[2,128,4,512]{3,1,2,0:T(8,128)S(1)} fusion(bf16[512,2,128,1]{0,2,3,1:T(8,128)(2,1)S(1)} %bitcast.273, f32[2,512,512,4]{2,1,3,0:T(8,128)} %get-tuple-element.33, f32[2,4,512]{2,1,0:T(4,128)S(1)} %bitcast.285, pred[512,512]{0,1:T(8,128)(4,1)S(1)} %get-tuple-element.21), kind=kOutput, calls=%fused_computation.79 | convolution fusion | flops 545259520 | bytes 11026432 | tf_op jit(solution)/shard_map/hgqk,khd->qhgd/dot_general | solution.py:97
  50.6 3.2 %multiply_reduce_fusion = (f32[512,2,4]{0,2,1:T(4,128)S(1)}, bf16[512,2,4,128]{0,3,2,1:T(8,128)(2,1)}) fusion(bf16[512,1024]{0,1:T(8,128)(2,1)S(1)} %copy.61, bf16[512,2,128,1]{0,2,3,1:T(8,128)(2,1)S(1)} %bitcast.264, f32[2,512,512,4]{2,1,3,0:T(8,128)S(1)} %get-tuple-element.29, f32[2,4,512]{2,1,0:T(4,128)S(1)} %bitcast.286, ...), kind=kOutput, calls=%fused_computation.45 | convolution fusion | flops 548925440 | bytes 15237120 | tf_op jit(solution)/shard_map/hgqk,khd->qhgd/dot_general | solution.py:97
  53.8 3.0 %fusion.1 = bf16[2,4,512,512]{2,3,1,0:T(8,128)(2,1)S(1)} fusion(f32[2,512,512,4]{2,1,3,0:T(8,128)S(1)} %get-tuple-element.29, f32[2,4,512]{2,1,0:T(4,128)S(1)} %bitcast.291, f32[2,4,512]{2,1,0:T(4,128)S(1)} %bitcast.287, pred[512,512]{0,1:T(8,128)(4,1)S(1)} %get-tuple-element.22, bf16[512,2,128,1]{0,2,3,1:T(8,128)(2,1)S(1)} %bitcast.265, ...), kind=kOutput, calls=%fused_computation.2 | convolution fusion | flops 549453824 | bytes 14188544 | tf_op jit(solution)/shard_map/qhgd,khd->hgqk/dot_general | solution.py:115
  56.8 7.9 %fusion.3 = bf16[2,4,512,512]{2,3,1,0:T(8,128)(2,1)} fusion(f32[2,512,512,4]{2,1,3,0:T(8,128)} %get-tuple-element.33, f32[2,4,512]{2,1,0:T(4,128)S(1)} %bitcast.292, f32[2,4,512]{2,1,0:T(4,128)S(1)} %bitcast.288, pred[512,512]{0,1:T(8,128)(4,1)S(1)} %get-tuple-element.21, bf16[512,2,128,1]{0,2,3,1:T(8,128)(2,1)S(1)} %bitcast.274, ...), kind=kOutput, calls=%fused_computation.5 | convolution fusion | flops 549453824 | bytes 14188544 | tf_op jit(solution)/shard_map/qhgd,khd->hgqk/dot_general | solution.py:115
  64.7 4.3 %fusion.5 = bf16[2,4,512,512]{2,3,1,0:T(8,128)(2,1)} fusion(f32[2,512,512,4]{2,1,3,0:T(8,128)S(1)} %get-tuple-element.31, f32[2,4,512]{2,1,0:T(4,128)S(1)} %bitcast.293, f32[2,4,512]{2,1,0:T(4,128)S(1)} %bitcast.289, pred[512,512]{0,1:T(8,128)(4,1)S(1)} %get-tuple-element.23, bf16[512,2,128,1]{0,2,3,1:T(8,128)(2,1)S(1)} %copy-done.11, ...), kind=kOutput, calls=%fused_computation.8 | convolution fusion | flops 549453824 | bytes 14188544 | tf_op jit(solution)/shard_map/qhgd,khd->hgqk/dot_general | solution.py:115
  69.0 1.5 %fusion.30 = f32[2,512,128]{1,2,0:T(8,128)S(1)} fusion(bf16[2,4,512,512]{2,3,1,0:T(8,128)(2,1)S(1)} %fusion.1, bf16[512,2,4,128]{0,3,2,1:T(8,128)(2,1)S(1)} %bitcast.246), kind=kOutput, calls=%fused_computation.50 | convolution fusion | flops 537001984 | bytes 5767168 | tf_op jit(solution)/shard_map/hgqk,qhgd->khd/dot_general | solution.py:124
  70.7 1.2 %copy.81 = f32[1,512,256]{2,1,0:T(8,128)S(1)} copy(f32[1,512,256]{1,2,0:T(8,128)} %bitcast.271) | data formatting | bytes 1048576 | tf_op jit(solution)/shard_map/stack;reshape | solution.py:132
  71.9 1.0 pad_maximum_fusion
  73.0 7.0 %collective-permute-start.2 = (f32[2,512,256]{2,1,0:T(8,128)}, f32[2,512,256]{2,1,0:T(8,128)}, u32[]{:S(2)}, u32[]{:S(2)}) collective-permute-start(f32[2,512,256]{2,1,0:T(8,128)} %pad_maximum_fusion), channel_id=1, source_target_pairs={{4,0},{8,4},{12,8},{16,12},{20,16},{24,20},{28,24},{5,1},{9,5},{13... | collective-permute-start | bytes 3145736 | tf_op jit(solution)/shard_map/ppermute | solution.py:19
  80.0 1.0 copy.86
  81.0 3.7 %fusion.31 = f32[2,512,128]{1,2,0:T(8,128)S(1)} fusion(bf16[2,4,512,512]{2,3,1,0:T(8,128)(2,1)} %fusion.3, bf16[512,2,4,128]{0,3,2,1:T(8,128)(2,1)S(1)} %bitcast.247), kind=kOutput, calls=%fused_computation.51 | convolution fusion | flops 537001984 | bytes 5767168 | tf_op jit(solution)/shard_map/hgqk,qhgd->khd/dot_general | solution.py:124
  84.7 1.0 copy.85
  85.7 3.0 %fusion.47 = f32[2,4,512,128]{2,3,1,0:T(8,128)S(1)} fusion(bf16[512,2,128,1]{0,2,3,1:T(8,128)(2,1)} %copy-done.5, bf16[2,4,512,512]{2,3,1,0:T(8,128)(2,1)} %fusion.5), kind=kOutput, calls=%fused_computation.85 | convolution fusion | flops 536870912 | bytes 6553600 | tf_op jit(solution)/shard_map/hgqk,khd->qhgd/dot_general | solution.py:120
  88.7 6.4 %fusion.40 = f32[2,512,128,1]{1,2,3,0:T(8,128)} fusion(bf16[512,2,4,128]{0,3,2,1:T(8,128)(2,1)} %bitcast.255, f32[2,512,512,4]{2,1,3,0:T(8,128)} %copy-done, f32[2,4,512]{2,1,0:T(4,128)S(1)} %bitcast.290, pred[512,512]{0,1:T(8,128)(4,1)S(1)} %get-tuple-element.23), kind=kOutput, calls=%fused_computation.80 | convolution fusion | flops 545259520 | bytes 10240000 | tf_op jit(solution)/shard_map/hgqk,qhgd->khd/dot_general | solution.py:129
  95.2 2.4 %maximum_add_fusion.1 = f32[2,512,256]{2,1,0:T(8,128)} fusion(f32[2,512,256]{2,1,0:T(8,128)} %collective-permute-done.2, f32[1,512,256]{2,1,0:T(8,128)S(1)} %copy-done.9, f32[1,512,256]{2,1,0:T(8,128)S(1)} %copy-done.10), kind=kLoop, calls=%fused_computation.55 | loop fusion | flops 524288 | bytes 3145728 | tf_op jit(solution)/shard_map/add | solution.py:148
  97.6 2.3 %collective-permute-start.3 = (f32[2,512,256]{2,1,0:T(8,128)}, f32[2,512,256]{2,1,0:T(8,128)}, u32[]{:S(2)}, u32[]{:S(2)}) collective-permute-start(f32[2,512,256]{2,1,0:T(8,128)} %maximum_add_fusion.1), channel_id=1, source_target_pairs={{4,0},{8,4},{12,8},{16,12},{20,16},{24,20},{28,24},{5,1},{9,5},{13... | collective-permute-start | bytes 3145736 | tf_op jit(solution)/shard_map/ppermute | solution.py:19
  99.9 2.3 %fusion.29 = f32[2,512,128]{1,2,0:T(8,128)} fusion(bf16[2,4,512,512]{2,3,1,0:T(8,128)(2,1)S(1)} %copy-done.3, bf16[512,2,4,128]{0,3,2,1:T(8,128)(2,1)S(1)} %bitcast.248), kind=kOutput, calls=%fused_computation.49 | convolution fusion | flops 537001984 | bytes 5767168 | tf_op jit(solution)/shard_map/hgqk,qhgd->khd/dot_general | solution.py:124
  102.1 2.0 %copy.75 = f32[1,512,256]{2,1,0:T(8,128)} copy(f32[1,512,256]{1,2,0:T(8,128)} %bitcast.261) | data formatting | bytes 1048576 | tf_op jit(solution)/shard_map/stack;reshape | solution.py:132
  104.2 2.0 %copy.76 = f32[1,512,256]{2,1,0:T(8,128)} copy(f32[1,512,256]{1,2,0:T(8,128)} %bitcast.272) | data formatting | bytes 1048576 | tf_op jit(solution)/shard_map/stack;reshape | solution.py:132
  106.2 3.1 %fusion.46 = f32[2,128,4,512]{3,1,2,0:T(8,128)S(1)} fusion(bf16[512,2,128,1]{0,2,3,1:T(8,128)(2,1)} %bitcast.260, bf16[2,4,512,512]{2,3,1,0:T(8,128)(2,1)} %fusion.3), kind=kOutput, calls=%fused_computation.84 | convolution fusion | flops 536870912 | bytes 6553600 | tf_op jit(solution)/shard_map/hgqk,khd->qhgd/dot_general | solution.py:120
  109.4 0.4 copy-done.2
  109.8 1.1 fusion.27
  110.8 1.3 %copy.88 = bf16[512,1024]{1,0:T(8,128)(2,1)} copy(bf16[512,1024]{0,1:T(8,128)(2,1)S(1)} %bitcast.249) | data formatting | bytes 2097152
  112.2 2.3 %copy.87 = bf16[512,1024]{1,0:T(8,128)(2,1)} copy(bf16[512,1024]{0,1:T(8,128)(2,1)} %bitcast.256) | data formatting | bytes 2097152
  114.4 1.6 %fusion.32 = bf16[2,512,256]{2,1,0:T(8,128)(2,1)S(1)} fusion(f32[2,512,256]{2,1,0:T(8,128)} %collective-permute-done.3, f32[1,512,256]{2,1,0:T(8,128)} %copy.76, f32[1,512,256]{2,1,0:T(8,128)} %copy.75), kind=kLoop, calls=%fused_computation.53 | loop fusion | flops 786432 | bytes 2621440 | tf_op jit(solution)/shard_map/convert.1
  116.0 0.8 slice_bitcast_fusion
  (36 shorter events, 0.6 us)
Async XLA Ops:
  3.7 15.0 %collective-permute-start.1 = (bf16[2,512,256]{1,2,0:T(8,128)(2,1)}, bf16[2,512,256]{1,2,0:T(8,128)(2,1)}, u32[]{:S(2)}, u32[]{:S(2)}) collective-permute-start(bf16[2,512,256]{1,2,0:T(8,128)(2,1)} %pad_maximum_fusion.1), channel_id=1, source_target_pairs={{0,8},{4,12},{8,16},{12,20},{16,24},{20,28},{1,9},{5,13},{9,17},{1... | collective-permute-start | bytes 1572872 | tf_op jit(solution)/shard_map/ppermute | solution.py:19
  5.0 16.8 %collective-permute-start = (bf16[2,512,256]{1,2,0:T(8,128)(2,1)}, bf16[2,512,256]{1,2,0:T(8,128)(2,1)}, u32[]{:S(2)}, u32[]{:S(2)}) collective-permute-start(bf16[2,512,256]{1,2,0:T(8,128)(2,1)} %pad_maximum_fusion.1), channel_id=1, source_target_pairs={{0,4},{4,8},{8,12},{12,16},{16,20},{20,24},{24,28},{1,5},{5,9},{9,... | collective-permute-start | bytes 1572872 | tf_op jit(solution)/shard_map/ppermute | solution.py:19
  12.2 9.5 %copy-start.5 = (bf16[512,2,128,1]{0,2,3,1:T(8,128)(2,1)}, bf16[512,2,128,1]{0,2,3,1:T(8,128)(2,1)S(1)}, u32[]{:S(2)}) copy-start(bf16[512,2,128,1]{0,2,3,1:T(8,128)(2,1)S(1)} %copy.101) | copy-start | bytes 786436
  14.6 50.2 %copy-start.4 = (bf16[512,1024]{0,1:T(8,128)(2,1)}, bf16[512,1024]{0,1:T(8,128)(2,1)S(1)}, u32[]{:S(2)}) copy-start(bf16[512,1024]{0,1:T(8,128)(2,1)S(1)} %copy.61) | copy-start | bytes 3145732
  16.2 48.5 %copy-start = (f32[2,512,512,4]{2,1,3,0:T(8,128)}, f32[2,512,512,4]{2,1,3,0:T(8,128)S(1)}, u32[]{:S(2)}) copy-start(f32[2,512,512,4]{2,1,3,0:T(8,128)S(1)} %get-tuple-element.31) | copy-start | bytes 25165828
  20.1 7.5 %copy-start.6 = (bf16[1,512,256]{1,2,0:T(8,128)(2,1)}, bf16[1,512,256]{1,2,0:T(8,128)(2,1)S(1)}, u32[]{:S(2)}) copy-start(bf16[1,512,256]{1,2,0:T(8,128)(2,1)S(1)} %get-tuple-element.18) | copy-start | bytes 786436
  22.8 12.2 %copy-start.8 = (bf16[1,512,256]{1,2,0:T(8,128)(2,1)}, bf16[1,512,256]{1,2,0:T(8,128)(2,1)S(1)}, u32[]{:S(2)}) copy-start(bf16[1,512,256]{1,2,0:T(8,128)(2,1)S(1)} %get-tuple-element.19) | copy-start | bytes 786436
  37.8 5.3 %copy-start.11 = (bf16[512,2,128,1]{0,2,3,1:T(8,128)(2,1)S(1)}, bf16[512,2,128,1]{0,2,3,1:T(8,128)(2,1)}, u32[]{:S(2)}) copy-start(bf16[512,2,128,1]{0,2,3,1:T(8,128)(2,1)} %copy.93) | copy-start | bytes 786436
  56.8 12.2 %copy-start.1 = (bf16[2,4,512,512]{2,3,1,0:T(8,128)(2,1)}, bf16[2,4,512,512]{2,3,1,0:T(8,128)(2,1)S(1)}, u32[]{:S(2)}) copy-start(bf16[2,4,512,512]{2,3,1,0:T(8,128)(2,1)S(1)} %fusion.1) | copy-start | bytes 12582916
  73.0 22.2 %collective-permute-start.2 = (f32[2,512,256]{2,1,0:T(8,128)}, f32[2,512,256]{2,1,0:T(8,128)}, u32[]{:S(2)}, u32[]{:S(2)}) collective-permute-start(f32[2,512,256]{2,1,0:T(8,128)} %pad_maximum_fusion), channel_id=1, source_target_pairs={{4,0},{8,4},{12,8},{16,12},{20,16},{24,20},{28,24},{5,1},{9,5},{13... | collective-permute-start | bytes 3145736 | tf_op jit(solution)/shard_map/ppermute | solution.py:19
  88.7 6.5 %copy-start.9 = (f32[1,512,256]{2,1,0:T(8,128)S(1)}, f32[1,512,256]{2,1,0:T(8,128)}, u32[]{:S(2)}) copy-start(f32[1,512,256]{2,1,0:T(8,128)} %copy.86) | copy-start | bytes 1572868
  88.7 6.5 %copy-start.10 = (f32[1,512,256]{2,1,0:T(8,128)S(1)}, f32[1,512,256]{2,1,0:T(8,128)}, u32[]{:S(2)}) copy-start(f32[1,512,256]{2,1,0:T(8,128)} %copy.85) | copy-start | bytes 1572868
  88.7 11.2 %copy-start.3 = (bf16[2,4,512,512]{2,3,1,0:T(8,128)(2,1)S(1)}, bf16[2,4,512,512]{2,3,1,0:T(8,128)(2,1)}, u32[]{:S(2)}) copy-start(bf16[2,4,512,512]{2,3,1,0:T(8,128)(2,1)} %fusion.5) | copy-start | bytes 12582916
  95.1 14.2 %copy-start.7 = (bf16[1,512,256]{1,2,0:T(8,128)(2,1)S(1)}, bf16[1,512,256]{1,2,0:T(8,128)(2,1)}, u32[]{:S(2)}) copy-start(bf16[1,512,256]{1,2,0:T(8,128)(2,1)} %copy-done.6) | copy-start | bytes 786436
  97.6 16.8 %collective-permute-start.3 = (f32[2,512,256]{2,1,0:T(8,128)}, f32[2,512,256]{2,1,0:T(8,128)}, u32[]{:S(2)}, u32[]{:S(2)}) collective-permute-start(f32[2,512,256]{2,1,0:T(8,128)} %maximum_add_fusion.1), channel_id=1, source_target_pairs={{4,0},{8,4},{12,8},{16,12},{20,16},{24,20},{28,24},{5,1},{9,5},{13... | collective-permute-start | bytes 3145736 | tf_op jit(solution)/shard_map/ppermute | solution.py:19
  106.2 3.5 %copy-start.2 = (bf16[2,4,512,512]{2,3,1,0:T(8,128)(2,1)S(1)}, bf16[2,4,512,512]{2,3,1,0:T(8,128)(2,1)}, u32[]{:S(2)}) copy-start(bf16[2,4,512,512]{2,3,1,0:T(8,128)(2,1)} %copy-done.1) | copy-start | bytes 12582916
where the time goes:
time: 118 us; the launch traced here: 117 us
  matrix products  62.9 us (53%)
  local copies, waits for them, and re-layouts  24.1 us (20%)
  other arithmetic  14.5 us (12%)
  starting transfers between devices  11.8 us (10%)
  waiting for transfers between devices  2.48 us (2%)
    dot_general x3, matrix products, back_fn(): jnp.einsum('qhgd,khd->hgqk', grad_split, value_split, preferred_element_t...  15.2 us
    dot_general x3, matrix products, back_fn(): jnp.einsum('hgqk,qhgd->khd', probs16[offset], grad_split, preferred_eleme...  14.5 us
    ppermute x4, starting transfers between devices, from_behind(): return lax.ppermute(block, axis, route)  11.8 us
    dot_general x3, matrix products, apply_fn(): jnp.einsum('hgqk,khd->qhgd', probs16[offset], value_split, preferred_elem...  10.7 us
    dot_general x3, matrix products, score_fn(): jnp.einsum('qhgd,khd->hgqk', query_split, key_split, preferred_element_ty...  8.02 us
    unnamed x29, local copies, waits for them, and re-layouts  7.68 us
    another operation x6, local copies, waits for them, and re-layouts, back_fn(): jnp.stack([key_term.reshape(length_dev, kv_heads * HD), value_term.reshap...  7.56 us
    reduce_sum x1, other arithmetic, body(): jnp.sum(jnp.where(masks[o], jnp.exp(scores[o] - highest), 0.0), axis=-1,...  7.4 us
  transfers between devices with their start and end apart: 4, of which 1 were waited for; matrix products, arithmetic and copies ran while one was open for 36% of the time, Pallas kernels for 0%

commit v1 on v0

v1 whole, which is shorter than its diff:
```python
import functools

import jax
import jax.numpy as jnp
from jax import lax
from jax.experimental import pallas as pl
from jax.experimental.pallas import tpu as pltpu
from jax.sharding import PartitionSpec as P

QH = 32
KVH = 8
HD = 128
BLK = 128
MOST_BLK = 8
GROUP = QH // KVH
SCALE = HD ** (-0.5)
WIDE = GROUP * HD
LOG2E = 1.4426950408889634
SCALE2 = SCALE * LOG2E
negative_fill = -1e30
F32 = jnp.float32
BF16 = jnp.bfloat16


def turn(block, step):
    n = lax.axis_size("ctx")
    return lax.ppermute(block, "ctx", [(i, (i + step) % n) for i in range(n)])


def dot(a, b):
    return lax.dot_general(a, b, (((1,), (0,)), ((), ())), preferred_element_type=F32)


def dot_nt(a, b):
    return lax.dot_general(a, b, (((1,), (1,)), ((), ())), preferred_element_type=F32)


def stack_heads(x):
    return jnp.concatenate([x[:, g * HD : (g + 1) * HD] for g in range(GROUP)], axis=0).T


def spread_heads(x):
    x = x.T
    rows = x.shape[0] // GROUP
    return jnp.concatenate([x[g * rows : (g + 1) * rows] for g in range(GROUP)], axis=1)


def blocks_behind(docs_ref, index):
    doc = docs_ref[index]
    count = jnp.int32(0)
    for d in range(1, MOST_BLK):
        same = (index >= d) & (docs_ref[jnp.maximum(index - d, 0)] == doc)
        count = count + jnp.where(same, 1, 0)
    return count


def crossing(docs_ref, base, blocks_dev):
    behind = blocks_behind(docs_ref, base)
    here = jnp.int32(0)
    for i in range(blocks_dev):
        here = here + jnp.where(docs_ref[base + i] == docs_ref[base], 1, 0)
    return behind, jnp.where(behind > 0, here, 0)


def biased(s, first, start):
    parts = []
    for b in range(s.shape[0] // BLK):
        bias = jnp.where(first + b >= start, 0.0, negative_fill).astype(F32)
        parts.append(s[b * BLK : (b + 1) * BLK] * SCALE2 + bias)
    return parts


def causal(part):
    key = lax.broadcasted_iota(jnp.int32, part.shape, 0)
    query = lax.broadcasted_iota(jnp.int32, part.shape, 1) % BLK
    return jnp.where(key <= query, part, negative_fill)


def own_scores(k, q_t, i, behind):
    parts = biased(dot(k[: (i + 1) * BLK], q_t), 0, i - behind)
    parts[i] = causal(parts[i])
    return jnp.concatenate(parts, axis=0)


def delta_of(o16, g_t):
    return jnp.sum(o16.astype(F32) * g_t.astype(F32), axis=0, keepdims=True)


class Store:
    def __init__(self, blocks, sem, whole, head):
        self.blocks, self.sem, self.whole, self.head = blocks, sem, whole, head

    def copy(self, i):
        place = self.whole.at[pl.ds(i * BLK, BLK), pl.ds(self.head * WIDE, WIDE)]
        return pltpu.make_async_copy(self.blocks.at[i], place, self.sem.at[i])

    def put(self, i, x):
        self.blocks[i] = x
        self.copy(i).start()


def own_part(blocks_dev, head, docs_ref, q_ref, g_ref, k_ref, v_ref, att_ref, qt_ref, gt_ref, stats_ref, o_ref, out_ref, sem):
    attended = Store(out_ref, sem, att_ref, head)
    base = lax.axis_index("ctx") * blocks_dev
    wide, slim = slice(head * WIDE, (head + 1) * WIDE), slice(head * HD, (head + 1) * HD)
    k = k_ref[:, slim]
    v_t = v_ref[:, slim].T
    for i in range(blocks_dev):
        rows = slice(i * BLK, (i + 1) * BLK)
        q_t = stack_heads(q_ref[rows, wide])
        g_t = stack_heads(g_ref[rows, wide])
        qt_ref[i] = q_t
        gt_ref[i] = g_t
        s = own_scores(k, q_t, i, blocks_behind(docs_ref, base + i))
        m = jnp.max(s, axis=0, keepdims=True)
        p = jnp.exp2(s - m)
        l = jnp.sum(p, axis=0, keepdims=True)
        o = dot(v_t[:, : (i + 1) * BLK], p.astype(BF16))
        o_ref[i] = o
        o16 = (o * (1.0 / l)).astype(BF16)
        attended.put(i, spread_heads(o16))
        for r, row in enumerate((m, l, m + jnp.log2(l), delta_of(o16, g_t))):
            stats_ref[r * blocks_dev + i : r * blocks_dev + i + 1, :] = row
    for i in range(blocks_dev):
        attended.copy(i).wait()


def own_first(blocks_dev, heads, *refs):
    sources, att_ref, targets, outs = refs[:5], refs[5], refs[6:11], refs[11:15]
    out_ref, sem, docs_smem, read_sem = refs[15:]
    docs = pltpu.make_async_copy(sources[0], docs_smem, read_sem.at[0, 0])
    docs_out = pltpu.make_async_copy(sources[0], targets[0], read_sem.at[0, 1])
    reads = []
    for a in range(1, 5):
        width = sources[a].shape[1] // heads
        for h in range(heads):
            part = (slice(None), pl.ds(h * width, width))
            reads.append((h, pltpu.make_async_copy(sources[a].at[part], targets[a].at[part], read_sem.at[a, h])))
    reads.sort(key=lambda read: read[0])
    docs.start()
    for _, read in reads:
        read.start()
    docs_out.start()
    docs.wait()
    for h, read in reads:
        if h == 0:
            read.wait()
    own_part(blocks_dev, 0, docs_smem, *targets[1:], att_ref, *outs, out_ref, sem)
    for h, read in reads:
        if h > 0:
            read.wait()
    docs_out.wait()


def own_later(blocks_dev, head, docs_ref, q_ref, g_ref, k_ref, v_ref, _, *rest):
    own_part(blocks_dev, head, docs_ref, q_ref, g_ref, k_ref, v_ref, *rest)


def far_part(blocks_dev, head, docs_ref, qt_ref, gt_ref, k1_ref, v1_ref, k2_ref, v2_ref, stats_ref, o0_ref, _, *rest):
    att_ref, dq_ref, ls_ref, d1_ref, d2_ref, acc_k, acc_v, out_ref, sem = rest
    far = k2_ref.shape[0] // BLK
    reach = blocks_dev + far
    behind, here = crossing(docs_ref, lax.axis_index("ctx") * blocks_dev, blocks_dev)
    start = reach - behind
    head_cols = slice(head * HD, (head + 1) * HD)
    attended = Store(out_ref, sem, att_ref, head)
    ls_ref[...] = stats_ref[2 * blocks_dev :, :]
    d1_ref[...] = jnp.zeros_like(d1_ref)
    d2_ref[...] = jnp.zeros_like(d2_ref)

    def pair(lo, first, most):
        def keys(near_ref, far_ref):
            piece = near_ref[:, head_cols]
            if lo < far:
                piece = jnp.concatenate([far_ref[lo * BLK :, head_cols], piece], axis=0)
            return piece

        k, v = keys(k1_ref, k2_ref), keys(v1_ref, v2_ref)
        k_t, v_t = k.T, v.T
        blocks = range(first, min(first + 2, most))
        q_t = [qt_ref[i] for i in blocks]
        g_t = [gt_ref[i] for i in blocks]
        scores = [dot(k, q) for q in q_t]
        ps, p16s, outs, dps = [], [], [], []
        for j, i in enumerate(blocks):
            row = lambda r, i=i: stats_ref[r * blocks_dev + i : r * blocks_dev + i + 1, :]
            first_key = jnp.where(i < here, start, reach)
            s = jnp.concatenate(biased(scores[j], lo, first_key), axis=0)
            m = jnp.maximum(row(0), jnp.max(s, axis=0, keepdims=True))
            p = jnp.exp2(s - m)
            shrink = jnp.exp2(row(0) - m)
            l = row(1) * shrink + jnp.sum(p, axis=0, keepdims=True)
            inv = 1.0 / l
            p = p * inv
            ps.append(p)
            p16s.append(p.astype(BF16))
            ls_ref[i : i + 1, :] = m + jnp.log2(l)
            outs.append(dot(v_t, p16s[j]) + o0_ref[i] * (shrink * inv))
            dps.append(dot(v, g_t[j]))
        dss = []
        for j, i in enumerate(blocks):
            o16 = outs[j].astype(BF16)
            delta = delta_of(o16, g_t[j])
            ls_ref[blocks_dev + i : blocks_dev + i + 1, :] = delta
            dss.append((ps[j] * (dps[j] - delta)).astype(BF16))
            dq_ref[i] = dot(k_t, dss[j])
            attended.put(i, spread_heads(o16))
        dv = dot_nt(jnp.concatenate(g_t, axis=1), jnp.concatenate(p16s, axis=1))
        dk = dot_nt(jnp.concatenate(q_t, axis=1), jnp.concatenate(dss, axis=1))
        if first:
            acc_v[:, lo * BLK :] += dv
            acc_k[:, lo * BLK :] += dk
        else:
            acc_v[:, lo * BLK :] = dv
            acc_k[:, lo * BLK :] = dk

    def rectangle(lo, most):
        pair(lo, 0, most)
        for first in range(2, most, 2):

            @pl.when(here > first)
            def _(first=first):
                pair(lo, first, most)

        for i in range(most):

            @pl.when(here > i // 2 * 2)
            def _(i=i):
                attended.copy(i).wait()

        for c, acc, scale in ((0, acc_k, SCALE), (1, acc_v, 1.0)):
            whole = (acc[:, lo * BLK :] * scale).astype(BF16).T
            cols = slice(c * HD, (c + 1) * HD)
            if lo < far:
                d2_ref[lo * BLK :, cols] = whole[: (far - lo) * BLK]
            d1_ref[:, cols] = whole[(far - lo) * BLK :]

    @pl.when((here > 0) & (start >= far))
    def _():
        rectangle(far, blocks_dev)

    if far >= 1:

        @pl.when((here > 0) & (start == far - 1))
        def _():
            rectangle(far - 1, min(blocks_dev, MOST_BLK - blocks_dev - 1))

    if far >= 2:

        @pl.when((here > 0) & (start < far - 1))
        def _():
            rectangle(0, min(blocks_dev, MOST_BLK - blocks_dev - 2))


def own_backward(blocks_dev, heads, docs_ref, k_ref, v_ref, *rest):
    given, (query_ref, *outs), scratch = rest[: 4 * heads], rest[4 * heads : 6 * heads + 1], rest[6 * heads + 1 :]
    acc_k, acc_v, out_ref, sem = scratch
    base = lax.axis_index("ctx") * blocks_dev
    _, here = crossing(docs_ref, base, blocks_dev)
    for h in range(heads):
        qt_ref, gt_ref, ls_ref, dq_ref = given[4 * h : 4 * h + 4]
        store = Store(out_ref.at[h], sem.at[h], query_ref, h)
        k, v = k_ref[:, h * HD : (h + 1) * HD], v_ref[:, h * HD : (h + 1) * HD]
        k_t = k.T
        acc_k[h] = jnp.zeros_like(acc_k[h])
        acc_v[h] = jnp.zeros_like(acc_v[h])
        for i in range(blocks_dev):
            n = (i + 1) * BLK
            q_t, g_t = qt_ref[i], gt_ref[i]
            s = own_scores(k, q_t, i, blocks_behind(docs_ref, base + i))
            p = jnp.exp2(s - ls_ref[i : i + 1, :])
            acc_v[h, :, :n] += dot_nt(g_t, p.astype(BF16))
            ds = (p * (dot(v[:n], g_t) - ls_ref[blocks_dev + i : blocks_dev + i + 1, :])).astype(BF16)
            acc_k[h, :, :n] += dot_nt(q_t, ds)
            dq = dot(k_t[:, :n], ds) + jnp.where(i < here, dq_ref[i], 0.0)
            store.put(i, spread_heads((dq * SCALE).astype(BF16)))
        outs[2 * h][...] = (acc_k[h] * SCALE).T
        outs[2 * h + 1][...] = acc_v[h].T
    for h in range(heads):
        for i in range(blocks_dev):
            Store(out_ref.at[h], sem.at[h], query_ref, h).copy(i).wait()


def finish(heads, *refs):
    dk_out, dv_out = refs[4 * heads :]
    for h in range(heads):
        dk_ref, dv_ref, near_ref, far_ref = refs[4 * h : 4 * h + 4]
        skip = dk_ref.shape[0] - far_ref.shape[0]
        for out, own_ref, cols in ((dk_out, dk_ref, slice(0, HD)), (dv_out, dv_ref, slice(HD, 2 * HD))):
            whole = own_ref[...] + near_ref[:, cols].astype(F32)
            out[:skip, h * HD : (h + 1) * HD] = whole[:skip].astype(BF16)
            whole = whole[skip:] + far_ref[:, cols].astype(F32)
            out[skip:, h * HD : (h + 1) * HD] = whole.astype(BF16)


def body(queries, key_vecs, value_vecs, out_grad, doc_ids):
    length_dev = queries.shape[0]
    blocks_dev = length_dev // BLK
    heads = key_vecs.shape[1] // HD
    lanes = GROUP * BLK
    far = (MOST_BLK - 1 - blocks_dev) * BLK
    tile = (blocks_dev, HD, lanes)
    part = (length_dev, HD)
    out_blocks = [pltpu.VMEM((blocks_dev, BLK, WIDE), BF16), pltpu.SemaphoreType.DMA((blocks_dev,))]

    def call(kernel, args, outs, scratch=(), hbm_args=(), hbm_outs=(), alias=None):
        vmem = pl.BlockSpec(memory_space=pltpu.VMEM)
        smem = pl.BlockSpec(memory_space=pltpu.SMEM)
        hbm = pl.BlockSpec(memory_space=pltpu.HBM)
        return pl.pallas_call(
            kernel,
            in_specs=[hbm if i in hbm_args else smem if x.dtype == jnp.int32 else vmem for i, x in enumerate(args)],
            out_specs=[hbm if i in hbm_outs else vmem for i in range(len(outs))],
            out_shape=[jax.ShapeDtypeStruct(*out) for out in outs],
            scratch_shapes=scratch,
            input_output_aliases=alias or {},
            compiler_params=pltpu.CompilerParams(vmem_limit_bytes=24 << 20),
        )(*args)

    k1 = turn(key_vecs, 1)
    v1 = turn(value_vecs, 1)
    inputs = [pltpu.with_memory_space_constraint(x, pltpu.HBM) for x in (doc_ids, queries, out_grad, key_vecs, value_vecs)]
    per_head = [(tile, BF16), (tile, BF16), ((4 * blocks_dev, lanes), F32), (tile, F32)]
    attended, doc_ids, queries, out_grad, key_vecs, value_vecs, *outs = call(
        functools.partial(own_first, blocks_dev, heads),
        inputs,
        [(queries.shape, BF16), *((x.shape, x.dtype) for x in inputs), *per_head],
        [*out_blocks, pltpu.SMEM(doc_ids.shape, jnp.int32), pltpu.SemaphoreType.DMA((5, max(heads, 2)))],
        hbm_args=range(5),
        hbm_outs=(0,),
    )
    k1, outs[0] = lax.optimization_barrier((k1, outs[0]))
    k2 = turn(k1[length_dev - far :], 1)
    v2 = turn(v1[length_dev - far :], 1)
    first = [outs]
    for h in range(1, heads):
        args = [doc_ids, queries, out_grad, key_vecs, value_vecs, attended]
        attended, *outs = call(
            functools.partial(own_later, blocks_dev, h),
            args,
            [(queries.shape, BF16), *per_head],
            out_blocks,
            hbm_args=(5,),
            hbm_outs=(0,),
            alias={5: 0},
        )
        first.append(outs)

    given, returned = [], []
    for h in range(heads):
        q_t, g_t, stats, o0 = first[h]
        args = [doc_ids, q_t, g_t, k1, v1, k2, v2, stats, o0, attended]
        attended, dq, ls, d1, d2 = call(
            functools.partial(far_part, blocks_dev, h),
            args,
            [
                (queries.shape, BF16),
                (tile, F32),
                ((2 * blocks_dev, lanes), F32),
                ((length_dev, 2 * HD), BF16),
                ((far, 2 * HD), BF16),
            ],
            [pltpu.VMEM((HD, length_dev + far), F32)] * 2 + out_blocks,
            hbm_args=(len(args) - 1,),
            hbm_outs=(0,),
            alias={len(args) - 1: 0},
        )
        given += [q_t, g_t, ls, dq]
        d1 = turn(d1, -1)
        d2 = turn(d2, -2)
        returned.append((d1, d2))

    query_grad, *own = call(
        functools.partial(own_backward, blocks_dev, heads),
        [doc_ids, key_vecs, value_vecs, *given],
        [(queries.shape, BF16)] + [(part, F32)] * (2 * heads),
        [pltpu.VMEM((heads, HD, length_dev), F32)] * 2
        + [pltpu.VMEM((heads, blocks_dev, BLK, WIDE), BF16), pltpu.SemaphoreType.DMA((heads, blocks_dev))],
        hbm_outs=(0,),
    )
    args = [x for h in range(heads) for x in (*own[2 * h : 2 * h + 2], *returned[h])]
    key_grad, value_grad = call(functools.partial(finish, heads), args, [(key_vecs.shape, BF16)] * 2)
    return (attended, query_grad, key_grad, value_grad)


def solution(mesh):
    placed = (P("ctx", "tp"), P("ctx", "tp"), P("ctx", "tp"), P("ctx", "tp"), P())
    return jax.shard_map(
        body,
        mesh=mesh,
        in_specs=placed,
        out_specs=(P("ctx", "tp"), P("ctx", "tp"), P("ctx", "tp"), P("ctx", "tp")),
        check_vma=False,
    )
```

time: 118 us -> 46.7 us (0.40)
  the two profiles are of different devices: /device:TPU:25 before, /device:TPU:0 now
where the time goes in v1:
time: 46.7 us; the launch traced here: 46.5 us
  starting transfers between devices  15.6 us (33%)
  Pallas kernels  15.3 us (33%)
  waiting for transfers between devices  14.9 us (32%)
  between operations  0.7 us (1%)
    ppermute x8, starting transfers between devices, turn(): return lax.ppermute(block, 'ctx', [(i, (i + step) % n) for i in range(n)])  15.6 us
    pallas_call x6, Pallas kernels, call(): pl.pallas_call(kernel, in_specs=[hbm if i in hbm_args else smem if x.dtyp...  15.3 us
    ppermute x8, waiting for transfers between devices, turn(): return lax.ppermute(block, 'ctx', [(i, (i + step) % n) for i in range(n)])  14.9 us
  transfers between devices with their start and end apart: 8, of which 6 were waited for; matrix products, arithmetic and copies ran while one was open for 0% of the time, Pallas kernels for 27%

profile of v1, /device:TPU:0, one launch (start us, length us, event | category | flops | bytes accessed | tf_op | source)
XLA Modules:
  0.0 46.5 jit_solution(14370866805368355452)
XLA Ops:
  0.6 0.5 %collective-permute-start.1 = (bf16[512,256]{1,0:T(8,128)(2,1)}, bf16[512,256]{1,0:T(8,128)(2,1)S(1)}, u32[]{:S(2)}, u32[]{:S(2)}) collective-permute-start(bf16[512,256]{1,0:T(8,128)(2,1)} %refs_4_.1), channel_id=1, source_target_pairs={{0,4},{4,8},{8,12},{12,16},{16,20},{20,24},{24,28},{28,0},{1,5},{5... | collective-permute-start | bytes 786440 | tf_op jit(solution)/shard_map/ppermute | solution.py:27
  1.2 2.7 %collective-permute-start = (bf16[512,256]{1,0:T(8,128)(2,1)}, bf16[512,256]{1,0:T(8,128)(2,1)S(1)}, u32[]{:S(2)}, u32[]{:S(2)}) collective-permute-start(bf16[512,256]{1,0:T(8,128)(2,1)} %refs_3_.1), channel_id=1, source_target_pairs={{0,4},{4,8},{8,12},{12,16},{16,20},{20,24},{24,28},{28,0},{1,5},{5... | collective-permute-start | bytes 786440 | tf_op jit(solution)/shard_map/ppermute | solution.py:27
  3.9 3.8 %shard_map.84 = (bf16[512,1024]{1,0:T(8,128)(2,1)}, s32[32]{0:T(128)S(1)}, bf16[512,1024]{1,0:T(8,128)(2,1)S(1)}, bf16[512,1024]{1,0:T(8,128)(2,1)S(1)}, bf16[51...) custom-call(s32[32]{0:T(128)} %refs_0_.1, ...), custom_call_target="tpu_custom_call" | custom-call | tf_op jit(solution)/shard_map/pallas_call | solution.py:310
  7.7 1.8 %collective-permute-done.1.v1_ref = bf16[512,256]{1,0:T(8,128)(2,1)S(1)} collective-permute-done((bf16[512,256]{1,0:T(8,128)(2,1)}, bf16[512,256]{1,0:T(8,128)(2,1)S(1)}, u32[]{:S(2)}, u32[]{:S(2)}) %collective-permute-start.1) | collective-permute-done | bytes 262176 | tf_op jit(solution)/shard_map/ppermute | solution.py:27
  9.5 0.1 collective-permute-start.3
  9.6 2.7 %collective-permute-done.k1_ref = bf16[512,256]{1,0:T(8,128)(2,1)S(1)} collective-permute-done((bf16[512,256]{1,0:T(8,128)(2,1)}, bf16[512,256]{1,0:T(8,128)(2,1)S(1)}, u32[]{:S(2)}, u32[]{:S(2)}) %collective-permute-start) | collective-permute-done | bytes 262176 | tf_op jit(solution)/shard_map/ppermute | solution.py:27
  12.3 0.1 collective-permute-start.2
  12.4 3.0 %shard_map.85 = (bf16[512,1024]{1,0:T(8,128)(2,1)}, bf16[4,128,512]{2,1,0:T(8,128)(2,1)S(1)}, bf16[4,128,512]{2,1,0:T(8,128)(2,1)S(1)}, f32[16,512]{1,0:T(8,128)S(1)}, f32[4,128,512]{2,1,0:T(8,128)S(1)}) custom-call(s32[32]{0:T(128)S(1)} %get-tuple-element.38.docs_ref, ...), custom_call_target="tpu_custom_call", output_to_operand_aliasing={{0}: (5, {})} | custom-call | tf_op jit(solution)/shard_map/pallas_call | solution.py:310
  15.4 1.1 %collective-permute-done.3.v2_ref = bf16[384,256]{1,0:T(8,128)(2,1)S(1)} collective-permute-done((bf16[384,256]{1,0:T(8,128)(2,1)S(1)}, bf16[384,256]{1,0:T(8,128)(2,1)S(1)}, u32[]{:S(2)}, u32[]{:S(2)}) %collective-permute-start.3) | collective-permute-done | bytes 196640 | tf_op jit(solution)/shard_map/ppermute | solution.py:27
  16.4 2.8 %collective-permute-done.2.k2_ref = bf16[384,256]{1,0:T(8,128)(2,1)S(1)} collective-permute-done((bf16[384,256]{1,0:T(8,128)(2,1)S(1)}, bf16[384,256]{1,0:T(8,128)(2,1)S(1)}, u32[]{:S(2)}, u32[]{:S(2)}) %collective-permute-start.2) | collective-permute-done | bytes 196640 | tf_op jit(solution)/shard_map/ppermute | solution.py:27
  19.2 0.8 %shard_map.86 = (bf16[512,1024]{1,0:T(8,128)(2,1)}, f32[4,128,512]{2,1,0:T(8,128)S(1)}, f32[8,512]{1,0:T(8,128)S(1)}, bf16[512,256]{1,0:T(8,128)(2,1)S(1)}, bf16[384,256]{1,0:T(8,128)(2,1)S(1)}) custom-call(s32[32]{0:T(128)S(1)} %get-tuple-element.38.docs_ref, ...), custom_call_target="tpu_custom_call", output_to_operand_aliasing={{0}: (9, {})} | custom-call | tf_op jit(solution)/shard_map/pallas_call | solution.py:310
  20.1 0.9 %shard_map.87 = (bf16[512,1024]{1,0:T(8,128)(2,1)}, f32[4,128,512]{2,1,0:T(8,128)S(1)}, f32[8,512]{1,0:T(8,128)S(1)}, bf16[512,256]{1,0:T(8,128)(2,1)S(1)}, bf16[384,256]{1,0:T(8,128)(2,1)S(1)}) custom-call(s32[32]{0:T(128)S(1)} %get-tuple-element.38.docs_ref, ...), custom_call_target="tpu_custom_call", output_to_operand_aliasing={{0}: (9, {})} | custom-call | tf_op jit(solution)/shard_map/pallas_call | solution.py:310
  20.9 5.8 %collective-permute-start.6 = (bf16[512,256]{1,0:T(8,128)(2,1)S(1)}, bf16[512,256]{1,0:T(8,128)(2,1)S(1)}, u32[]{:S(2)}, u32[]{:S(2)}) collective-permute-start(bf16[512,256]{1,0:T(8,128)(2,1)S(1)} %get-tuple-element.68), channel_id=1, source_target_pairs={{0,28},{4,0},{8,4},{12,8},{16,12},{20,16},{24,20},{28,24},{1,29},{... | collective-permute-start | bytes 786440 | tf_op jit(solution)/shard_map/ppermute | solution.py:27
  26.7 4.2 %collective-permute-start.4 = (bf16[512,256]{1,0:T(8,128)(2,1)S(1)}, bf16[512,256]{1,0:T(8,128)(2,1)S(1)}, u32[]{:S(2)}, u32[]{:S(2)}) collective-permute-start(bf16[512,256]{1,0:T(8,128)(2,1)S(1)} %get-tuple-element.64), channel_id=1, source_target_pairs={{0,28},{4,0},{8,4},{12,8},{16,12},{20,16},{24,20},{28,24},{1,29},{... | collective-permute-start | bytes 786440 | tf_op jit(solution)/shard_map/ppermute | solution.py:27
  30.9 0.9 %collective-permute-start.7 = (bf16[384,256]{1,0:T(8,128)(2,1)S(1)}, bf16[384,256]{1,0:T(8,128)(2,1)S(1)}, u32[]{:S(2)}, u32[]{:S(2)}) collective-permute-start(bf16[384,256]{1,0:T(8,128)(2,1)S(1)} %get-tuple-element.69), channel_id=1, source_target_pairs={{0,24},{4,28},{8,0},{12,4},{16,8},{20,12},{24,16},{28,20},{1,25},{... | collective-permute-start | bytes 589832 | tf_op jit(solution)/shard_map/ppermute | solution.py:27
  31.9 1.3 %collective-permute-start.5 = (bf16[384,256]{1,0:T(8,128)(2,1)S(1)}, bf16[384,256]{1,0:T(8,128)(2,1)S(1)}, u32[]{:S(2)}, u32[]{:S(2)}) collective-permute-start(bf16[384,256]{1,0:T(8,128)(2,1)S(1)} %get-tuple-element.65), channel_id=1, source_target_pairs={{0,24},{4,28},{8,0},{12,4},{16,8},{20,12},{24,16},{28,20},{1,25},{... | collective-permute-start | bytes 589832 | tf_op jit(solution)/shard_map/ppermute | solution.py:27
  33.2 5.9 %shard_map.88 = (bf16[512,1024]{1,0:T(8,128)(2,1)}, f32[512,128]{1,0:T(8,128)S(1)}, f32[512,128]{1,0:T(8,128)S(1)}, f32[512,128]{1,0:T(8,128)S(1)}, f32[512,128]{1,0:T(8,128)S(1)}) custom-call(s32[32]{0:T(128)S(1)} %get-tuple-element.38.docs_ref, bf16[512,256]{1,0:T(8,128)(2,1)S(1)} %get-tuple-element.41.k_ref, ...), custom_call_target="tpu_custom_call" | custom-call | tf_op jit(solution)/shard_map/pallas_call | solution.py:310
  39.1 4.4 %collective-permute-done.7.refs_7_ = bf16[384,256]{1,0:T(8,128)(2,1)S(1)} collective-permute-done((bf16[384,256]{1,0:T(8,128)(2,1)S(1)}, bf16[384,256]{1,0:T(8,128)(2,1)S(1)}, u32[]{:S(2)}, u32[]{:S(2)}) %collective-permute-start.7) | collective-permute-done | bytes 196640 | tf_op jit(solution)/shard_map/ppermute | solution.py:27
  43.5 2.1 %collective-permute-done.5.refs_3_ = bf16[384,256]{1,0:T(8,128)(2,1)S(1)} collective-permute-done((bf16[384,256]{1,0:T(8,128)(2,1)S(1)}, bf16[384,256]{1,0:T(8,128)(2,1)S(1)}, u32[]{:S(2)}, u32[]{:S(2)}) %collective-permute-start.5) | collective-permute-done | bytes 196640 | tf_op jit(solution)/shard_map/ppermute | solution.py:27
  45.6 0.0 collective-permute-done.6.refs_6_
  45.6 0.0 collective-permute-done.4.refs_2_
  45.6 0.9 %shard_map.89 = (bf16[512,256]{1,0:T(8,128)(2,1)}, bf16[512,256]{1,0:T(8,128)(2,1)}) custom-call(f32[512,128]{1,0:T(8,128)S(1)} %get-tuple-element.62.refs_0_, f32[512,128]{1,0:T(8,128)S(1)} %get-tuple-element.63.refs_1_, bf16[512,256]{1,0:T(8,128)(2,1)S(1)} %collective-permute-done.4.refs_2_, bf16[384,256]{1,0:T(8,128)(2,1)S(1)} %collective-permute-done.5.refs_3_, ...), custom_call_target="tpu_custom_call" | custom-call | tf_op jit(solution)/shard_map/pallas_call | solution.py:310
  (2 shorter events, 0.0 us)
Async XLA Ops:
  0.6 8.8 %collective-permute-start.1 = (bf16[512,256]{1,0:T(8,128)(2,1)}, bf16[512,256]{1,0:T(8,128)(2,1)S(1)}, u32[]{:S(2)}, u32[]{:S(2)}) collective-permute-start(bf16[512,256]{1,0:T(8,128)(2,1)} %refs_4_.1), channel_id=1, source_target_pairs={{0,4},{4,8},{8,12},{12,16},{16,20},{20,24},{24,28},{28,0},{1,5},{5... | collective-permute-start | bytes 786440 | tf_op jit(solution)/shard_map/ppermute | solution.py:27
  1.2 11.1 %collective-permute-start = (bf16[512,256]{1,0:T(8,128)(2,1)}, bf16[512,256]{1,0:T(8,128)(2,1)S(1)}, u32[]{:S(2)}, u32[]{:S(2)}) collective-permute-start(bf16[512,256]{1,0:T(8,128)(2,1)} %refs_3_.1), channel_id=1, source_target_pairs={{0,4},{4,8},{8,12},{12,16},{16,20},{20,24},{24,28},{28,0},{1,5},{5... | collective-permute-start | bytes 786440 | tf_op jit(solution)/shard_map/ppermute | solution.py:27
  9.5 6.9 %collective-permute-start.3 = (bf16[384,256]{1,0:T(8,128)(2,1)S(1)}, bf16[384,256]{1,0:T(8,128)(2,1)S(1)}, u32[]{:S(2)}, u32[]{:S(2)}) collective-permute-start(bf16[384,256]{1,0:T(8,128)(2,1)S(1)} %slice.8), channel_id=1, source_target_pairs={{0,4},{4,8},{8,12},{12,16},{16,20},{20,24},{24,28},{28,0},{1,5},{5... | collective-permute-start | bytes 589832 | tf_op jit(solution)/shard_map/ppermute | solution.py:27
  12.3 6.9 %collective-permute-start.2 = (bf16[384,256]{1,0:T(8,128)(2,1)S(1)}, bf16[384,256]{1,0:T(8,128)(2,1)S(1)}, u32[]{:S(2)}, u32[]{:S(2)}) collective-permute-start(bf16[384,256]{1,0:T(8,128)(2,1)S(1)} %slice.6), channel_id=1, source_target_pairs={{0,4},{4,8},{8,12},{12,16},{16,20},{20,24},{24,28},{28,0},{1,5},{5... | collective-permute-start | bytes 589832 | tf_op jit(solution)/shard_map/ppermute | solution.py:27
  20.9 24.7 %collective-permute-start.6 = (bf16[512,256]{1,0:T(8,128)(2,1)S(1)}, bf16[512,256]{1,0:T(8,128)(2,1)S(1)}, u32[]{:S(2)}, u32[]{:S(2)}) collective-permute-start(bf16[512,256]{1,0:T(8,128)(2,1)S(1)} %get-tuple-element.68), channel_id=1, source_target_pairs={{0,28},{4,0},{8,4},{12,8},{16,12},{20,16},{24,20},{28,24},{1,29},{... | collective-permute-start | bytes 786440 | tf_op jit(solution)/shard_map/ppermute | solution.py:27
  26.7 18.9 %collective-permute-start.4 = (bf16[512,256]{1,0:T(8,128)(2,1)S(1)}, bf16[512,256]{1,0:T(8,128)(2,1)S(1)}, u32[]{:S(2)}, u32[]{:S(2)}) collective-permute-start(bf16[512,256]{1,0:T(8,128)(2,1)S(1)} %get-tuple-element.64), channel_id=1, source_target_pairs={{0,28},{4,0},{8,4},{12,8},{16,12},{20,16},{24,20},{28,24},{1,29},{... | collective-permute-start | bytes 786440 | tf_op jit(solution)/shard_map/ppermute | solution.py:27
  30.9 12.5 %collective-permute-start.7 = (bf16[384,256]{1,0:T(8,128)(2,1)S(1)}, bf16[384,256]{1,0:T(8,128)(2,1)S(1)}, u32[]{:S(2)}, u32[]{:S(2)}) collective-permute-start(bf16[384,256]{1,0:T(8,128)(2,1)S(1)} %get-tuple-element.69), channel_id=1, source_target_pairs={{0,24},{4,28},{8,0},{12,4},{16,8},{20,12},{24,16},{28,20},{1,25},{... | collective-permute-start | bytes 589832 | tf_op jit(solution)/shard_map/ppermute | solution.py:27
  31.9 13.7 %collective-permute-start.5 = (bf16[384,256]{1,0:T(8,128)(2,1)S(1)}, bf16[384,256]{1,0:T(8,128)(2,1)S(1)}, u32[]{:S(2)}, u32[]{:S(2)}) collective-permute-start(bf16[384,256]{1,0:T(8,128)(2,1)S(1)} %get-tuple-element.65), channel_id=1, source_target_pairs={{0,24},{4,28},{8,0},{12,4},{16,8},{20,12},{24,16},{28,20},{1,25},{... | collective-permute-start | bytes 589832 | tf_op jit(solution)/shard_map/ppermute | solution.py:27

commit v2 on v1

--- a/solution.py
+++ b/solution.py
@@ -22,9 +22,9 @@
 BF16 = jnp.bfloat16
 
 
-def turn(block, step):
+def turn(block, step, around=True):
     n = lax.axis_size("ctx")
-    return lax.ppermute(block, "ctx", [(i, (i + step) % n) for i in range(n)])
+    return lax.ppermute(block, "ctx", [(i, (i + step) % n) for i in range(n) if around or 0 <= i + step < n])
 
 
 def dot(a, b):
@@ -156,100 +156,138 @@
     own_part(blocks_dev, head, docs_ref, q_ref, g_ref, k_ref, v_ref, *rest)
 
 
-def far_part(blocks_dev, head, docs_ref, qt_ref, gt_ref, k1_ref, v1_ref, k2_ref, v2_ref, stats_ref, o0_ref, _, *rest):
-    att_ref, dq_ref, ls_ref, d1_ref, d2_ref, acc_k, acc_v, out_ref, sem = rest
+def over_variants(docs_ref, blocks_dev, far, run):
+    behind, here = crossing(docs_ref, lax.axis_index("ctx") * blocks_dev, blocks_dev)
+    start = blocks_dev + far - behind
+    cases = [(far, blocks_dev, start >= far)]
+    if far >= 1:
+        cases.append((far - 1, min(blocks_dev, MOST_BLK - blocks_dev - 1), start == far - 1))
+    if far >= 2:
+        cases.append((0, min(blocks_dev, MOST_BLK - blocks_dev - 2), start < far - 1))
+    for lo, most, case in cases:
+
+        @pl.when((here > 0) & case)
+        def _(lo=lo, most=most):
+            run(lo, most, start, here)
+
+
+def window(near_ref, far_ref, cols, lo):
+    piece = near_ref[:, cols]
+    if lo * BLK < far_ref.shape[0]:
+        piece = jnp.concatenate([far_ref[lo * BLK :, cols], piece], axis=0)
+    return piece
+
+
+def in_pairs(most, here, run):
+    run(range(0, min(2, most)))
+    for first in range(2, most, 2):
+
+        @pl.when(here > first)
+        def _(first=first):
+            run(range(first, min(first + 2, most)))
+
+
+def give_back(acc, lo, far, scale, cols, near_ref, far_ref):
+    whole = (acc[:, lo * BLK :] * scale).astype(BF16).T
+    if lo < far:
+        far_ref[lo * BLK :, cols] = whole[: (far - lo) * BLK]
+    near_ref[:, cols] = whole[(far - lo) * BLK :]
+
+
+def accumulate(acc, lo, fresh, x):
+    if fresh:
+        acc[:, lo * BLK :] = x
+    else:
+        acc[:, lo * BLK :] += x
+
+
+def far_keys(blocks_dev, heads, docs_ref, k1_ref, k2_ref, *rest):
+    given, (near_ref, far_ref, *outs), acc = rest[: 3 * heads], rest[3 * heads : -1], rest[-1]
     far = k2_ref.shape[0] // BLK
     reach = blocks_dev + far
-    behind, here = crossing(docs_ref, lax.axis_index("ctx") * blocks_dev, blocks_dev)
-    start = reach - behind
-    head_cols = slice(head * HD, (head + 1) * HD)
-    attended = Store(out_ref, sem, att_ref, head)
-    ls_ref[...] = stats_ref[2 * blocks_dev :, :]
-    d1_ref[...] = jnp.zeros_like(d1_ref)
-    d2_ref[...] = jnp.zeros_like(d2_ref)
-
-    def pair(lo, first, most):
-        def keys(near_ref, far_ref):
-            piece = near_ref[:, head_cols]
-            if lo < far:
-                piece = jnp.concatenate([far_ref[lo * BLK :, head_cols], piece], axis=0)
-            return piece
-
-        k, v = keys(k1_ref, k2_ref), keys(v1_ref, v2_ref)
-        k_t, v_t = k.T, v.T
-        blocks = range(first, min(first + 2, most))
-        q_t = [qt_ref[i] for i in blocks]
-        g_t = [gt_ref[i] for i in blocks]
-        scores = [dot(k, q) for q in q_t]
-        ps, p16s, outs, dps = [], [], [], []
-        for j, i in enumerate(blocks):
-            row = lambda r, i=i: stats_ref[r * blocks_dev + i : r * blocks_dev + i + 1, :]
-            first_key = jnp.where(i < here, start, reach)
-            s = jnp.concatenate(biased(scores[j], lo, first_key), axis=0)
-            m = jnp.maximum(row(0), jnp.max(s, axis=0, keepdims=True))
-            p = jnp.exp2(s - m)
-            shrink = jnp.exp2(row(0) - m)
-            l = row(1) * shrink + jnp.sum(p, axis=0, keepdims=True)
-            inv = 1.0 / l
-            p = p * inv
-            ps.append(p)
-            p16s.append(p.astype(BF16))
-            ls_ref[i : i + 1, :] = m + jnp.log2(l)
-            outs.append(dot(v_t, p16s[j]) + o0_ref[i] * (shrink * inv))
-            dps.append(dot(v, g_t[j]))
-        dss = []
-        for j, i in enumerate(blocks):
-            o16 = outs[j].astype(BF16)
-            delta = delta_of(o16, g_t[j])
-            ls_ref[blocks_dev + i : blocks_dev + i + 1, :] = delta
-            dss.append((ps[j] * (dps[j] - delta)).astype(BF16))
-            dq_ref[i] = dot(k_t, dss[j])
-            attended.put(i, spread_heads(o16))
-        dv = dot_nt(jnp.concatenate(g_t, axis=1), jnp.concatenate(p16s, axis=1))
-        dk = dot_nt(jnp.concatenate(q_t, axis=1), jnp.concatenate(dss, axis=1))
-        if first:
-            acc_v[:, lo * BLK :] += dv
-            acc_k[:, lo * BLK :] += dk
-        else:
-            acc_v[:, lo * BLK :] = dv
-            acc_k[:, lo * BLK :] = dk
-
-    def rectangle(lo, most):
-        pair(lo, 0, most)
-        for first in range(2, most, 2):
-
-            @pl.when(here > first)
-            def _(first=first):
-                pair(lo, first, most)
-
-        for i in range(most):
-
-            @pl.when(here > i // 2 * 2)
-            def _(i=i):
-                attended.copy(i).wait()
-
-        for c, acc, scale in ((0, acc_k, SCALE), (1, acc_v, 1.0)):
-            whole = (acc[:, lo * BLK :] * scale).astype(BF16).T
-            cols = slice(c * HD, (c + 1) * HD)
-            if lo < far:
-                d2_ref[lo * BLK :, cols] = whole[: (far - lo) * BLK]
-            d1_ref[:, cols] = whole[(far - lo) * BLK :]
-
-    @pl.when((here > 0) & (start >= far))
-    def _():
-        rectangle(far, blocks_dev)
-
-    if far >= 1:
-
-        @pl.when((here > 0) & (start == far - 1))
-        def _():
-            rectangle(far - 1, min(blocks_dev, MOST_BLK - blocks_dev - 1))
-
-    if far >= 2:
-
-        @pl.when((here > 0) & (start < far - 1))
-        def _():
-            rectangle(0, min(blocks_dev, MOST_BLK - blocks_dev - 2))
+    near_ref[...] = jnp.zeros_like(near_ref)
+    far_ref[...] = jnp.zeros_like(far_ref)
+
+    def run(lo, most, start, here):
+        for h in range(heads):
+            qt_ref, gt_ref, stats_ref = given[3 * h : 3 * h + 3]
+            p_ref, rows_ref = outs[2 * h : 2 * h + 2]
+            cols = slice(h * HD, (h + 1) * HD)
+
+            def pair(blocks, qt_ref=qt_ref, gt_ref=gt_ref, stats_ref=stats_ref, p_ref=p_ref, rows_ref=rows_ref, cols=cols):
+                k = window(k1_ref, k2_ref, cols, lo)
+                scores = [dot(k, qt_ref[i]) for i in blocks]
+                weights = []
+                for s, i in zip(scores, blocks):
+                    m0 = stats_ref[i : i + 1, :]
+                    s = jnp.concatenate(biased(s, lo, jnp.where(i < here, start, reach)), axis=0)
+                    m = jnp.maximum(m0, jnp.max(s, axis=0, keepdims=True))
+                    p = jnp.exp2(s - m)
+                    shrink = jnp.exp2(m0 - m)
+                    l = stats_ref[blocks_dev + i : blocks_dev + i + 1, :] * shrink + jnp.sum(p, axis=0, keepdims=True)
+                    inv = 1.0 / l
+                    p16 = (p * inv).astype(BF16)
+                    p_ref[i, lo * BLK :, :] = p16
+                    weights.append(p16)
+                    rows_ref[i : i + 1, :] = m + jnp.log2(l)
+                    rows_ref[blocks_dev + i : blocks_dev + i + 1, :] = shrink * inv
+                g_t = jnp.concatenate([gt_ref[i] for i in blocks], axis=1)
+                accumulate(acc, lo, blocks[0] == 0, dot_nt(g_t, jnp.concatenate(weights, axis=1)))
+
+            in_pairs(most, here, pair)
+            give_back(acc, lo, far, 1.0, cols, near_ref, far_ref)
+
+    over_variants(docs_ref, blocks_dev, far, run)
+
+
+def far_values(blocks_dev, heads, docs_ref, k1_ref, k2_ref, v1_ref, v2_ref, *rest):
+    given, rest = rest[: 6 * heads], rest[6 * heads + 1 :]
+    (att_ref, near_ref, far_ref, *outs), (acc, out_ref, sem) = rest[:-3], rest[-3:]
+    far = k2_ref.shape[0] // BLK
+    near_ref[...] = jnp.zeros_like(near_ref)
+    far_ref[...] = jnp.zeros_like(far_ref)
+    for h in range(heads):
+        outs[2 * h + 1][...] = given[6 * h + 2][2 * blocks_dev :, :]
+
+    def run(lo, most, start, here):
+        for h in range(heads):
+            cols = slice(h * HD, (h + 1) * HD)
+            attended = Store(out_ref.at[h], sem.at[h], att_ref, h)
+
+            def pair(blocks, h=h, cols=cols, attended=attended):
+                qt_ref, gt_ref, _, o0_ref, p_ref, rows_ref = given[6 * h : 6 * h + 6]
+                dq_ref, ls_ref = outs[2 * h : 2 * h + 2]
+                k, v = window(k1_ref, k2_ref, cols, lo), window(v1_ref, v2_ref, cols, lo)
+                k_t, v_t = k.T, v.T
+                ps = [p_ref[i, lo * BLK :, :] for i in blocks]
+                grads = [gt_ref[i] for i in blocks]
+                keep = [rows_ref[blocks_dev + i : blocks_dev + i + 1, :] for i in blocks]
+                attended16 = [
+                    (dot(v_t, p) + o0_ref[i] * scale).astype(BF16) for p, i, scale in zip(ps, blocks, keep)
+                ]
+                dps = [dot(v, g) for g in grads]
+                dss = []
+                for p, dp, o16, g, i in zip(ps, dps, attended16, grads, blocks):
+                    delta = delta_of(o16, g)
+                    ls_ref[i : i + 1, :] = rows_ref[i : i + 1, :]
+                    ls_ref[blocks_dev + i : blocks_dev + i + 1, :] = delta
+                    ds = (p.astype(F32) * (dp - delta)).astype(BF16)
+                    dq_ref[i] = dot(k_t, ds)
+                    dss.append(ds)
+                    attended.put(i, spread_heads(o16))
+                q_t = jnp.concatenate([qt_ref[i] for i in blocks], axis=1)
+                accumulate(acc, lo, blocks[0] == 0, dot_nt(q_t, jnp.concatenate(dss, axis=1)))
+
+            in_pairs(most, here, pair)
+            give_back(acc, lo, far, SCALE, cols, near_ref, far_ref)
+        for h in range(heads):
+            for i in range(most):
+
+                @pl.when(here > i // 2 * 2)
+                def _(h=h, i=i):
+                    Store(out_ref.at[h], sem.at[h], att_ref, h).copy(i).wait()
+
+    over_variants(docs_ref, blocks_dev, far, run)
 
 
 def own_backward(blocks_dev, heads, docs_ref, k_ref, v_ref, *rest):
@@ -282,15 +320,15 @@
 
 
 def finish(heads, *refs):
-    dk_out, dv_out = refs[4 * heads :]
+    returned, (dk_out, dv_out) = refs[2 * heads : 2 * heads + 4], refs[2 * heads + 4 :]
     for h in range(heads):
-        dk_ref, dv_ref, near_ref, far_ref = refs[4 * h : 4 * h + 4]
-        skip = dk_ref.shape[0] - far_ref.shape[0]
-        for out, own_ref, cols in ((dk_out, dk_ref, slice(0, HD)), (dv_out, dv_ref, slice(HD, 2 * HD))):
+        cols = slice(h * HD, (h + 1) * HD)
+        for c, out in enumerate((dk_out, dv_out)):
+            own_ref, near_ref, far_ref = refs[2 * h + c], returned[2 * c], returned[2 * c + 1]
+            skip = own_ref.shape[0] - far_ref.shape[0]
             whole = own_ref[...] + near_ref[:, cols].astype(F32)
-            out[:skip, h * HD : (h + 1) * HD] = whole[:skip].astype(BF16)
-            whole = whole[skip:] + far_ref[:, cols].astype(F32)
-            out[skip:, h * HD : (h + 1) * HD] = whole.astype(BF16)
+            out[:skip, cols] = whole[:skip].astype(BF16)
+            out[skip:, cols] = (whole[skip:] + far_ref[:, cols].astype(F32)).astype(BF16)
 
 
 def body(queries, key_vecs, value_vecs, out_grad, doc_ids):
@@ -301,6 +339,7 @@
     far = (MOST_BLK - 1 - blocks_dev) * BLK
     tile = (blocks_dev, HD, lanes)
     part = (length_dev, HD)
+    key_grad_shape = key_vecs.shape
     out_blocks = [pltpu.VMEM((blocks_dev, BLK, WIDE), BF16), pltpu.SemaphoreType.DMA((blocks_dev,))]
 
     def call(kernel, args, outs, scratch=(), hbm_args=(), hbm_outs=(), alias=None):
@@ -331,7 +370,6 @@
     )
     k1, outs[0] = lax.optimization_barrier((k1, outs[0]))
     k2 = turn(k1[length_dev - far :], 1)
-    v2 = turn(v1[length_dev - far :], 1)
     first = [outs]
     for h in range(1, heads):
         args = [doc_ids, queries, out_grad, key_vecs, value_vecs, attended]
@@ -345,31 +383,40 @@
             alias={5: 0},
         )
         first.append(outs)
-
-    given, returned = [], []
-    for h in range(heads):
-        q_t, g_t, stats, o0 = first[h]
-        args = [doc_ids, q_t, g_t, k1, v1, k2, v2, stats, o0, attended]
-        attended, dq, ls, d1, d2 = call(
-            functools.partial(far_part, blocks_dev, h),
-            args,
-            [
-                (queries.shape, BF16),
-                (tile, F32),
-                ((2 * blocks_dev, lanes), F32),
-                ((length_dev, 2 * HD), BF16),
-                ((far, 2 * HD), BF16),
-            ],
-            [pltpu.VMEM((HD, length_dev + far), F32)] * 2 + out_blocks,
-            hbm_args=(len(args) - 1,),
-            hbm_outs=(0,),
-            alias={len(args) - 1: 0},
-        )
-        given += [q_t, g_t, ls, dq]
-        d1 = turn(d1, -1)
-        d2 = turn(d2, -2)
-        returned.append((d1, d2))
-
+    v1, first[-1][0] = lax.optimization_barrier((v1, first[-1][0]))
+    v2 = turn(v1[length_dev - far :], 1)
+
+    both = [((length_dev, heads * HD), BF16), ((far, heads * HD), BF16)]
+    acc = pltpu.VMEM((HD, length_dev + far), F32)
+    args = [doc_ids, k1, k2] + [x for q_t, g_t, stats, _ in first for x in (q_t, g_t, stats)]
+    near_v, far_v, *weights = call(
+        functools.partial(far_keys, blocks_dev, heads),
+        args,
+        both + [((blocks_dev, length_dev + far, lanes), BF16), ((2 * blocks_dev, lanes), F32)] * heads,
+        [acc],
+    )
+    near_v = turn(near_v, -1)
+    far_v = turn(far_v, -2, False)
+
+    args = [doc_ids, k1, k2, v1, v2] + [x for h in range(heads) for x in (*first[h], *weights[2 * h : 2 * h + 2])]
+    args.append(attended)
+    attended, near_k, far_k, *outs = call(
+        functools.partial(far_values, blocks_dev, heads),
+        args,
+        [(queries.shape, BF16), *both] + [(tile, F32), ((2 * blocks_dev, lanes), F32)] * heads,
+        [
+            acc,
+            pltpu.VMEM((heads, blocks_dev, BLK, WIDE), BF16),
+            pltpu.SemaphoreType.DMA((heads, blocks_dev)),
+        ],
+        hbm_args=(len(args) - 1,),
+        hbm_outs=(0,),
+        alias={len(args) - 1: 0},
+    )
+    near_k = turn(near_k, -1)
+    far_k = turn(far_k, -2)
+
+    given = [x for h in range(heads) for x in (*first[h][:2], outs[2 * h + 1], outs[2 * h])]
     query_grad, *own = call(
         functools.partial(own_backward, blocks_dev, heads),
         [doc_ids, key_vecs, value_vecs, *given],
@@ -378,8 +425,9 @@
         + [pltpu.VMEM((heads, blocks_dev, BLK, WIDE), BF16), pltpu.SemaphoreType.DMA((heads, blocks_dev))],
         hbm_outs=(0,),
     )
-    args = [x for h in range(heads) for x in (*own[2 * h : 2 * h + 2], *returned[h])]
-    key_grad, value_grad = call(functools.partial(finish, heads), args, [(key_vecs.shape, BF16)] * 2)
+    key_grad, value_grad = call(
+        functools.partial(finish, heads), [*own, near_k, far_k, near_v, far_v], [(key_grad_shape, BF16)] * 2
+    )
     return (attended, query_grad, key_grad, value_grad)
 
 

time: 46.7 us -> 42.9 us (0.919)
  starting transfers between devices: 15.6 us -> 12.7 us
  waiting for transfers between devices: 14.9 us -> 14 us
    ppermute x8, starting transfers between devices: 15.6 us -> 12.7 us  [turn(): lax.ppermute(block, 'ctx', [(i, (i + step) % n) for i in range(n) if arou...]
    ppermute x8, waiting for transfers between devices: 14.9 us -> 14 us  [turn(): lax.ppermute(block, 'ctx', [(i, (i + step) % n) for i in range(n) if arou...]
  transfers between devices with their start and end apart: 8 -> 8, of which waited for: 6 -> 5; matrix products, arithmetic and copies ran while one was open for 0% -> 0% of each run, Pallas kernels for 27% -> 32%
where the time goes in v2:
time: 42.9 us; the launch traced here: 42.7 us
  Pallas kernels  15.3 us (36%)
  waiting for transfers between devices  14 us (33%)
  starting transfers between devices  12.7 us (30%)
  between operations  0.71 us (2%)
    pallas_call x6, Pallas kernels, call(): pl.pallas_call(kernel, in_specs=[hbm if i in hbm_args else smem if x.dtyp...  15.3 us
    ppermute x8, waiting for transfers between devices, turn(): lax.ppermute(block, 'ctx', [(i, (i + step) % n) for i in range(n) if arou...  14 us
    ppermute x8, starting transfers between devices, turn(): lax.ppermute(block, 'ctx', [(i, (i + step) % n) for i in range(n) if arou...  12.7 us
  transfers between devices with their start and end apart: 8, of which 5 were waited for; matrix products, arithmetic and copies ran while one was open for 0% of the time, Pallas kernels for 32%

profile of v2, /device:TPU:0, one launch (start us, length us, event | category | flops | bytes accessed | tf_op | source)
XLA Modules:
  0.0 42.7 jit_solution(966146837368512249)
XLA Ops:
  0.6 0.5 %collective-permute-start = (bf16[512,256]{1,0:T(8,128)(2,1)}, bf16[512,256]{1,0:T(8,128)(2,1)S(1)}, u32[]{:S(2)}, u32[]{:S(2)}) collective-permute-start(bf16[512,256]{1,0:T(8,128)(2,1)} %refs_3_.1), channel_id=1, source_target_pairs={{0,4},{4,8},{8,12},{12,16},{16,20},{20,24},{24,28},{28,0},{1,5},{5... | collective-permute-start | bytes 786440 | tf_op jit(solution)/shard_map/ppermute | solution.py:27
  1.2 2.7 %collective-permute-start.2 = (bf16[512,256]{1,0:T(8,128)(2,1)}, bf16[512,256]{1,0:T(8,128)(2,1)S(1)}, u32[]{:S(2)}, u32[]{:S(2)}) collective-permute-start(bf16[512,256]{1,0:T(8,128)(2,1)} %refs_4_.1), channel_id=1, source_target_pairs={{0,4},{4,8},{8,12},{12,16},{16,20},{20,24},{24,28},{28,0},{1,5},{5... | collective-permute-start | bytes 786440 | tf_op jit(solution)/shard_map/ppermute | solution.py:27
  3.9 3.8 %shard_map.84 = (bf16[512,1024]{1,0:T(8,128)(2,1)}, s32[32]{0:T(128)S(1)}, bf16[512,1024]{1,0:T(8,128)(2,1)S(1)}, bf16[512,1024]{1,0:T(8,128)(2,1)S(1)}, bf16[51...) custom-call(s32[32]{0:T(128)} %refs_0_.1, ...), custom_call_target="tpu_custom_call" | custom-call | tf_op jit(solution)/shard_map/pallas_call | solution.py:349
  7.7 1.8 %collective-permute-done.k1_ref = bf16[512,256]{1,0:T(8,128)(2,1)S(1)} collective-permute-done((bf16[512,256]{1,0:T(8,128)(2,1)}, bf16[512,256]{1,0:T(8,128)(2,1)S(1)}, u32[]{:S(2)}, u32[]{:S(2)}) %collective-permute-start) | collective-permute-done | bytes 262176 | tf_op jit(solution)/shard_map/ppermute | solution.py:27
  9.5 0.1 collective-permute-start.1
  9.6 3.0 %shard_map.85 = (bf16[512,1024]{1,0:T(8,128)(2,1)}, bf16[4,128,512]{2,1,0:T(8,128)(2,1)S(1)}, bf16[4,128,512]{2,1,0:T(8,128)(2,1)S(1)}, f32[16,512]{1,0:T(8,128)S(1)}, f32[4,128,512]{2,1,0:T(8,128)S(1)}) custom-call(s32[32]{0:T(128)S(1)} %get-tuple-element.43.docs_ref, ...), custom_call_target="tpu_custom_call", output_to_operand_aliasing={{0}: (5, {})} | custom-call | tf_op jit(solution)/shard_map/pallas_call | solution.py:349
  12.6 0.0 collective-permute-done.2.v1_ref
  12.6 0.4 collective-permute-start.3
  13.0 3.4 %collective-permute-done.1.k2_ref = bf16[384,256]{1,0:T(8,128)(2,1)S(1)} collective-permute-done((bf16[384,256]{1,0:T(8,128)(2,1)S(1)}, bf16[384,256]{1,0:T(8,128)(2,1)S(1)}, u32[]{:S(2)}, u32[]{:S(2)}) %collective-permute-start.1) | collective-permute-done | bytes 196640 | tf_op jit(solution)/shard_map/ppermute | solution.py:27
  16.4 0.8 %shard_map.86 = (bf16[512,256]{1,0:T(8,128)(2,1)S(1)}, bf16[384,256]{1,0:T(8,128)(2,1)S(1)}, bf16[4,896,512]{2,1,0:T(8,128)(2,1)S(1)}, f32[8,512]{1,0:T(8,128)S(...) custom-call(s32[32]{0:T(128)S(1)} %get-tuple-element.43.docs_ref, ...), custom_call_target="tpu_custom_call" | custom-call | tf_op jit(solution)/shard_map/pallas_call | solution.py:349
  17.2 2.3 %collective-permute-done.3.v2_ref = bf16[384,256]{1,0:T(8,128)(2,1)S(1)} collective-permute-done((bf16[384,256]{1,0:T(8,128)(2,1)S(1)}, bf16[384,256]{1,0:T(8,128)(2,1)S(1)}, u32[]{:S(2)}, u32[]{:S(2)}) %collective-permute-start.3) | collective-permute-done | bytes 196640 | tf_op jit(solution)/shard_map/ppermute | solution.py:27
  19.5 0.9 %shard_map.87 = (bf16[512,1024]{1,0:T(8,128)(2,1)}, bf16[512,256]{1,0:T(8,128)(2,1)S(1)}, bf16[384,256]{1,0:T(8,128)(2,1)S(1)}, f32[4,128,512]{2,1,0:T(8,128)S(1...) custom-call(s32[32]{0:T(128)S(1)} %get-tuple-element.43.docs_ref, ...), custom_call_target="tpu_custom_call", output_to_operand_aliasing={{0}: (17, {})} | custom-call | tf_op jit(solution)/shard_map/pallas_call | solution.py:349
  20.4 2.6 %collective-permute-start.4 = (bf16[512,256]{1,0:T(8,128)(2,1)S(1)}, bf16[512,256]{1,0:T(8,128)(2,1)S(1)}, u32[]{:S(2)}, u32[]{:S(2)}) collective-permute-start(bf16[512,256]{1,0:T(8,128)(2,1)S(1)} %get-tuple-element.76), channel_id=1, source_target_pairs={{0,28},{4,0},{8,4},{12,8},{16,12},{20,16},{24,20},{28,24},{1,29},{... | collective-permute-start | bytes 786440 | tf_op jit(solution)/shard_map/ppermute | solution.py:27
  23.0 4.0 %collective-permute-start.6 = (bf16[512,256]{1,0:T(8,128)(2,1)S(1)}, bf16[512,256]{1,0:T(8,128)(2,1)S(1)}, u32[]{:S(2)}, u32[]{:S(2)}) collective-permute-start(bf16[512,256]{1,0:T(8,128)(2,1)S(1)} %get-tuple-element.78), channel_id=1, source_target_pairs={{0,28},{4,0},{8,4},{12,8},{16,12},{20,16},{24,20},{28,24},{1,29},{... | collective-permute-start | bytes 786440 | tf_op jit(solution)/shard_map/ppermute | solution.py:27
  27.0 1.2 %collective-permute-start.5 = (bf16[384,256]{1,0:T(8,128)(2,1)S(1)}, bf16[384,256]{1,0:T(8,128)(2,1)S(1)}, u32[]{:S(2)}, u32[]{:S(2)}) collective-permute-start(bf16[384,256]{1,0:T(8,128)(2,1)S(1)} %get-tuple-element.77), channel_id=1, source_target_pairs={{0,24},{4,28},{8,0},{12,4},{16,8},{20,12},{24,16},{28,20},{1,25},{... | collective-permute-start | bytes 589832 | tf_op jit(solution)/shard_map/ppermute | solution.py:27
  28.2 1.3 %collective-permute-start.7 = (bf16[384,256]{1,0:T(8,128)(2,1)S(1)}, bf16[384,256]{1,0:T(8,128)(2,1)S(1)}, u32[]{:S(2)}, u32[]{:S(2)}) collective-permute-start(bf16[384,256]{1,0:T(8,128)(2,1)S(1)} %get-tuple-element.79), channel_id=1, source_target_pairs={{8,0},{12,4},{16,8},{20,12},{24,16},{28,20},{9,1},{13,5},{17,9},{2... | collective-permute-start | bytes 589832 | tf_op jit(solution)/shard_map/ppermute | solution.py:27
  29.5 5.9 %shard_map.88 = (bf16[512,1024]{1,0:T(8,128)(2,1)}, f32[512,128]{1,0:T(8,128)S(1)}, f32[512,128]{1,0:T(8,128)S(1)}, f32[512,128]{1,0:T(8,128)S(1)}, f32[512,128]{1,0:T(8,128)S(1)}) custom-call(s32[32]{0:T(128)S(1)} %get-tuple-element.43.docs_ref, bf16[512,256]{1,0:T(8,128)(2,1)S(1)} %get-tuple-element.48.k_ref, ...), custom_call_target="tpu_custom_call" | custom-call | tf_op jit(solution)/shard_map/pallas_call | solution.py:349
  35.4 4.3 %collective-permute-done.5.refs_5_ = bf16[384,256]{1,0:T(8,128)(2,1)S(1)} collective-permute-done((bf16[384,256]{1,0:T(8,128)(2,1)S(1)}, bf16[384,256]{1,0:T(8,128)(2,1)S(1)}, u32[]{:S(2)}, u32[]{:S(2)}) %collective-permute-start.5) | collective-permute-done | bytes 196640 | tf_op jit(solution)/shard_map/ppermute | solution.py:27
  39.7 2.1 %collective-permute-done.7.refs_7_ = bf16[384,256]{1,0:T(8,128)(2,1)S(1)} collective-permute-done((bf16[384,256]{1,0:T(8,128)(2,1)S(1)}, bf16[384,256]{1,0:T(8,128)(2,1)S(1)}, u32[]{:S(2)}, u32[]{:S(2)}) %collective-permute-start.7) | collective-permute-done | bytes 196640 | tf_op jit(solution)/shard_map/ppermute | solution.py:27
  41.8 0.0 collective-permute-done.4.refs_4_
  41.8 0.0 collective-permute-done.6.refs_6_
  41.8 0.9 %shard_map.89 = (bf16[512,256]{1,0:T(8,128)(2,1)}, bf16[512,256]{1,0:T(8,128)(2,1)}) custom-call(f32[512,128]{1,0:T(8,128)S(1)} %get-tuple-element.72.refs_0_, f32[512,128]{1,0:T(8,128)S(1)} %get-tuple-element.73.refs_1_, f32[512,128]{1,0:T(8,128)S(1)} %get-tuple-element.74.refs_2_, f32[512,128]{1,0:T(8,128)S(1)} %get-tuple-element.75.refs_3_, ...), custom_call_target="tpu_custom_call" | custom-call | tf_op jit(solution)/shard_map/pallas_call | solution.py:349
  (2 shorter events, 0.0 us)
Async XLA Ops:
  0.6 8.8 %collective-permute-start = (bf16[512,256]{1,0:T(8,128)(2,1)}, bf16[512,256]{1,0:T(8,128)(2,1)S(1)}, u32[]{:S(2)}, u32[]{:S(2)}) collective-permute-start(bf16[512,256]{1,0:T(8,128)(2,1)} %refs_3_.1), channel_id=1, source_target_pairs={{0,4},{4,8},{8,12},{12,16},{16,20},{20,24},{24,28},{28,0},{1,5},{5... | collective-permute-start | bytes 786440 | tf_op jit(solution)/shard_map/ppermute | solution.py:27
  1.2 11.4 %collective-permute-start.2 = (bf16[512,256]{1,0:T(8,128)(2,1)}, bf16[512,256]{1,0:T(8,128)(2,1)S(1)}, u32[]{:S(2)}, u32[]{:S(2)}) collective-permute-start(bf16[512,256]{1,0:T(8,128)(2,1)} %refs_4_.1), channel_id=1, source_target_pairs={{0,4},{4,8},{8,12},{12,16},{16,20},{20,24},{24,28},{28,0},{1,5},{5... | collective-permute-start | bytes 786440 | tf_op jit(solution)/shard_map/ppermute | solution.py:27
  9.5 6.9 %collective-permute-start.1 = (bf16[384,256]{1,0:T(8,128)(2,1)S(1)}, bf16[384,256]{1,0:T(8,128)(2,1)S(1)}, u32[]{:S(2)}, u32[]{:S(2)}) collective-permute-start(bf16[384,256]{1,0:T(8,128)(2,1)S(1)} %slice.6), channel_id=1, source_target_pairs={{0,4},{4,8},{8,12},{12,16},{16,20},{20,24},{24,28},{28,0},{1,5},{5... | collective-permute-start | bytes 589832 | tf_op jit(solution)/shard_map/ppermute | solution.py:27
  12.6 6.9 %collective-permute-start.3 = (bf16[384,256]{1,0:T(8,128)(2,1)S(1)}, bf16[384,256]{1,0:T(8,128)(2,1)S(1)}, u32[]{:S(2)}, u32[]{:S(2)}) collective-permute-start(bf16[384,256]{1,0:T(8,128)(2,1)S(1)} %slice.7), channel_id=1, source_target_pairs={{0,4},{4,8},{8,12},{12,16},{16,20},{20,24},{24,28},{28,0},{1,5},{5... | collective-permute-start | bytes 589832 | tf_op jit(solution)/shard_map/ppermute | solution.py:27
  20.4 21.4 %collective-permute-start.4 = (bf16[512,256]{1,0:T(8,128)(2,1)S(1)}, bf16[512,256]{1,0:T(8,128)(2,1)S(1)}, u32[]{:S(2)}, u32[]{:S(2)}) collective-permute-start(bf16[512,256]{1,0:T(8,128)(2,1)S(1)} %get-tuple-element.76), channel_id=1, source_target_pairs={{0,28},{4,0},{8,4},{12,8},{16,12},{20,16},{24,20},{28,24},{1,29},{... | collective-permute-start | bytes 786440 | tf_op jit(solution)/shard_map/ppermute | solution.py:27
  23.0 18.8 %collective-permute-start.6 = (bf16[512,256]{1,0:T(8,128)(2,1)S(1)}, bf16[512,256]{1,0:T(8,128)(2,1)S(1)}, u32[]{:S(2)}, u32[]{:S(2)}) collective-permute-start(bf16[512,256]{1,0:T(8,128)(2,1)S(1)} %get-tuple-element.78), channel_id=1, source_target_pairs={{0,28},{4,0},{8,4},{12,8},{16,12},{20,16},{24,20},{28,24},{1,29},{... | collective-permute-start | bytes 786440 | tf_op jit(solution)/shard_map/ppermute | solution.py:27
  27.0 12.7 %collective-permute-start.5 = (bf16[384,256]{1,0:T(8,128)(2,1)S(1)}, bf16[384,256]{1,0:T(8,128)(2,1)S(1)}, u32[]{:S(2)}, u32[]{:S(2)}) collective-permute-start(bf16[384,256]{1,0:T(8,128)(2,1)S(1)} %get-tuple-element.77), channel_id=1, source_target_pairs={{0,24},{4,28},{8,0},{12,4},{16,8},{20,12},{24,16},{28,20},{1,25},{... | collective-permute-start | bytes 589832 | tf_op jit(solution)/shard_map/ppermute | solution.py:27
  28.2 13.6 %collective-permute-start.7 = (bf16[384,256]{1,0:T(8,128)(2,1)S(1)}, bf16[384,256]{1,0:T(8,128)(2,1)S(1)}, u32[]{:S(2)}, u32[]{:S(2)}) collective-permute-start(bf16[384,256]{1,0:T(8,128)(2,1)S(1)} %get-tuple-element.79), channel_id=1, source_target_pairs={{8,0},{12,4},{16,8},{20,12},{24,16},{28,20},{9,1},{13,5},{17,9},{2... | collective-permute-start | bytes 589832 | tf_op jit(solution)/shard_map/ppermute | solution.py:27
